TPU v7x, 128 devices: a whole 4x4x4 slice. The times are simulated.
128 devices in a mesh: row: 8 (over y, core), col: 16 (over z, x).
Axes of the slice: x: 4, y: 4, z: 4, core: 2. Of those that a mesh axis runs over, the one named last changes fastest.
Arguments:
- noisy: float32 [2048, 16384], P('row', 'col'), may hold values from -7 to 7
- fidelity: float32 [2048, 16384], P('row', 'col'), may hold values from 2 to 20
Outputs:
- denoised: float32 [2048, 16384], P('row', 'col')
- dual: float32 [2, 2048, 16384], P(None, 'row', 'col')
- final_tau: float32 [], replicated
All inputs are finite; a program needn't handle non-finite values.
Results may differ from a plain program's by a relative error of at most 0.0001.
Values sent between devices are 32-bit elements; how exact they have to be, the bound alone decides.
A program may use at most 64 MiB of HBM per device.

v0:
```python
import jax
import jax.numpy as jnp
from jax import lax
from jax.sharding import Mesh
from jax.sharding import PartitionSpec as P

ITERS = 4
ROW = ("row_0", "row_1")
COL = ("col_0", "col_1")


first_tau = 0.35
step_product = 0.124
adapt_rate = 0.5
adapt_decay = 0.9
epsilon = 1e-06


def sent_to_all(shard, axis):
    copies = jnp.broadcast_to(shard, (lax.axis_size(axis), *shard.shape))
    return lax.all_to_all(copies, axis, split_axis=0, concat_axis=0, tiled=True)


def over_copies(shard, axis):
    everything = sent_to_all(shard, axis)
    return jnp.sum(everything, axis=0)


def over_axes(shard, axes):
    far, near = axes
    nearer = over_copies(shard, near)
    return over_copies(nearer, far)


def together(arrays, axis):
    vector, at, done = (jnp.concatenate([a.reshape(-1) for a in arrays]), 0, [])
    total = over_axes(vector, axis)
    for a in arrays:
        done.append(total[at : at + a.size].reshape(a.shape))
        at += a.size
    return tuple(done)


def passed_along(value, axis, steps):
    count = lax.axis_size(axis)
    initial, last = (max(0, -steps), min(count, count - steps))
    return lax.ppermute(value, axis, [(source, source + steps) for source in range(initial, last)])


def diff_rows(field, below, is_last):
    below = jnp.where(is_last, field[..., -1:, :], below)
    return jnp.concatenate([field[..., 1:, :], below], axis=-2) - field


def diff_cols(field, right, is_last):
    right = jnp.where(is_last, field[..., :, -1:], right)
    return jnp.concatenate([field[..., :, 1:], right], axis=-1) - field


def residual_total(primal_part, dual_part):
    return together((primal_part, dual_part), ("row_0", ("row_1", "col_0", "col_1")))


def on_device(noisy, fidelity):
    row_last = lax.axis_index(ROW) == lax.axis_size(ROW) - 1
    col_last = lax.axis_index(COL) == lax.axis_size(COL) - 1
    cells = jnp.float32(noisy.shape[0] * noisy.shape[1] * lax.axis_size(ROW) * lax.axis_size(COL))

    def gradient_iter(field):
        below = passed_along(field[:1, :], ROW, -1)
        right = passed_along(field[:, 0][None, :], COL, -1)
        return (diff_rows(field, below, row_last), diff_cols(field, right.T, col_last))

    current = noisy
    dual_x = jnp.zeros_like(noisy)
    dual_y = jnp.zeros_like(noisy)
    div_prev = jnp.zeros_like(noisy)
    tau = jnp.float32(first_tau)
    sigma = jnp.float32(step_product) / tau
    iter_x, iter_y = gradient_iter(noisy)
    grad_x, grad_y = (iter_x, iter_y)
    for step in range(ITERS):
        moved_x = dual_x + sigma * grad_x
        moved_y = dual_y + sigma * grad_y
        shrink = jnp.maximum(1.0, jnp.sqrt(moved_x * moved_x + moved_y * moved_y))
        new_x = moved_x / shrink
        new_y = moved_y / shrink
        above = passed_along(new_x[-1:, :], ROW, 1)
        left = passed_along(new_y[:, -1][None, :], COL, 1)
        part_x = new_x - jnp.concatenate([above, new_x[:-1]], axis=0)
        part_y = new_y - jnp.concatenate([left.T, new_y[:, :-1]], axis=1)
        div_new = part_x + part_y
        updated = (current + tau * div_new + tau * fidelity * noisy) / (1.0 + tau * fidelity)
        change = current - updated
        fresh_x, fresh_y = gradient_iter(updated)
        change_x = iter_x - fresh_x
        change_y = iter_y - fresh_y
        next_x = 2.0 * fresh_x - iter_x
        next_y = 2.0 * fresh_y - iter_y
        iter_x, iter_y = (fresh_x, fresh_y)
        primal_part = jnp.sum(jnp.abs(change / tau + div_prev - div_new))
        dual_part = jnp.sum(jnp.abs((dual_x - new_x) / sigma - change_x)) + jnp.sum(
            jnp.abs((dual_y - new_y) / sigma - change_y)
        )
        primal, dualres = residual_total(primal_part, dual_part)
        ratio = jnp.log((primal / cells + epsilon) / (dualres / cells + epsilon))
        tau = tau * jnp.exp(adapt_rate * adapt_decay**step * ratio / (1.0 + jnp.abs(ratio)))
        sigma = jnp.float32(step_product) / tau
        current = updated
        dual_x, dual_y = (new_x, new_y)
        div_prev = div_new
        grad_x, grad_y = (next_x, next_y)
    return (current, jnp.stack([dual_x, dual_y]), tau)


def solution(mesh):
    finer = Mesh(mesh.devices.reshape(4, 2, 4, 4), ("row_0", "row_1", "col_0", "col_1"))
    placed = (P(ROW, COL), P(ROW, COL))
    return jax.shard_map(
        on_device,
        mesh=finer,
        in_specs=placed,
        out_specs=(P(ROW, COL), P(None, ROW, COL), P()),
        check_vma=False,
    )
```

profile of v0, /device:TPU:1, one launch (start us, length us, event | category | flops | bytes accessed | tf_op | source)
XLA Modules:
  0.0 245.4 jit_solution(7782368943243498806)
XLA Ops:
  4.0 3.3 %collective-permute-start = (f32[1,1024]{0,1:T(8,128)S(1)}, f32[1,1024]{0,1:T(8,128)}, u32[]{:S(2)}, u32[]{:S(2)}) collective-permute-start(f32[1,1024]{0,1:T(8,128)S(1)} %copy.44), channel_id=1, source_target_pairs={{16,0},{32,16},{48,32},{64,48},{80,64},{96,80},{112,96},{17,1},{33... | collective-permute-start | bytes 12296 | tf_op jit(solution)/shard_map/ppermute | solution.py:47
  10.5 5.0 %collective-permute-done = f32[1,1024]{0,1:T(8,128)} collective-permute-done((f32[1,1024]{0,1:T(8,128)S(1)}, f32[1,1024]{0,1:T(8,128)}, u32[]{:S(2)}, u32[]{:S(2)}) %collective-permute-start) | collective-permute-done | bytes 4128 | tf_op jit(solution)/shard_map/ppermute | solution.py:47
  21.1 4.3 %collective-permute-start.3 = (f32[1,256]{1,0:T(1,128)S(1)}, f32[1,256]{1,0:T(1,128)S(1)}, u32[]{:S(2)}, u32[]{:S(2)}) collective-permute-start(f32[1,256]{1,0:T(1,128)S(1)} %slice_bitcast_fusion.7), channel_id=1, source_target_pairs={{0,1},{1,2},{2,3},{3,4},{4,5},{5,6},{6,7},{7,8},{8,9},{9,10},{10,1... | collective-permute-start | bytes 3080 | tf_op jit(solution)/shard_map/ppermute | solution.py:47
  25.4 2.5 %copy.51 = f32[256,1024]{0,1:T(8,128)} copy(f32[256,1024]{1,0:T(8,128)} %param.3) | data formatting | bytes 2097152 | tf_op args[1]
  27.9 3.6 %abs_reduce_fusion.9 = (f32[]{:T(128)}, f32[256,1024]{0,1:T(8,128)S(1)}, f32[256,1024]{0,1:T(8,128)}) fusion(f32[256,1024]{0,1:T(8,128)S(1)} %copy.50, f32[256,1024]{0,1:T(8,128)} %copy.51, f32[256,1024]{0,1:T(8,128)S(1)} %get-tuple-element.47, f32[256,1023]{0,1:T(8,128)S(1)} %bitcast.58, f32[256,1]{0,1:T(1,128)S(1)} %bitcast.66, ...), kind=kLoop, calls=%fused_computation.58 | loop fusion | flops 4456447 | bytes 8388612 | tf_op jit(solution)/shard_map/reduce_sum | solution.py:101
  33.3 3.6 %collective-permute-start.4 = (f32[1,1024]{0,1:T(8,128)S(1)}, f32[1,1024]{0,1:T(8,128)S(1)}, u32[]{:S(2)}, u32[]{:S(2)}) collective-permute-start(f32[1,1024]{0,1:T(8,128)S(1)} %slice.225), channel_id=1, source_target_pairs={{16,0},{32,16},{48,32},{64,48},{80,64},{96,80},{112,96},{17,1},{33... | collective-permute-start | bytes 12296 | tf_op jit(solution)/shard_map/ppermute | solution.py:47
  36.9 7.4 %collective-permute-done.4 = f32[1,1024]{0,1:T(8,128)S(1)} collective-permute-done((f32[1,1024]{0,1:T(8,128)S(1)}, f32[1,1024]{0,1:T(8,128)S(1)}, u32[]{:S(2)}, u32[]{:S(2)}) %collective-permute-start.4) | collective-permute-done | bytes 4128 | tf_op jit(solution)/shard_map/ppermute | solution.py:47
  44.5 2.8 %abs_reduce_fusion.7 = (f32[]{:T(128)}, f32[256,1024]{0,1:T(8,128)}, f32[]{:T(128)}, f32[256,1024]{0,1:T(8,128)}) fusion(f32[256,1024]{0,1:T(8,128)S(1)} %copy-done.26, f32[256,1024]{0,1:T(8,128)S(1)} %get-tuple-element.47, f32[256,1024]{0,1:T(8,128)S(1)} %get-tuple-element.41, f32[256,1]{0,1:T(1,128)S(1)} %broadcast_select_fusion.4, ...), kind=kLoop, calls=%fused_computation.56 | loop fusion | flops 4194302 | bytes 9437192 | tf_op jit(solution)/shard_map/reduce_sum | solution.py:102
  49.3 17.9 %all_to_all.48 = f32[32,1,2]{2,1,0:T(1,128)S(1)} all-to-all(f32[32,1,2]{2,1,0:T(1,128)S(1)} %broadcast_in_dim.24), channel_id=1, replica_groups=mesh['row_0'=4,'row_1'=2,'col_0'=4,'col_1'=4] {'row_1','col_0','col_1'}, dimensions={0} | all-to-all | bytes 512 | tf_op jit(solution)/shard_map/all_to_all | solution.py:21
  67.3 7.4 %all_to_all.49 = f32[4,1,2]{2,1,0:T(1,128)S(1)} all-to-all(f32[4,1,2]{2,1,0:T(1,128)S(1)} %broadcast_in_dim.25), channel_id=1, replica_groups=mesh['row_0'=4,'row_1'=2,'col_0'=4,'col_1'=4] {'row_0'}, dimensions={0} | all-to-all | bytes 64 | tf_op jit(solution)/shard_map/all_to_all | solution.py:21
  76.8 2.9 %fusion.16 = (f32[256,1024]{0,1:T(8,128)S(1)}, f32[256,1024]{0,1:T(8,128)S(1)}, f32[256,1024]{0,1:T(8,128)S(1)}) fusion(f32[256,1024]{0,1:T(8,128)S(1)} %get-tuple-element.47, f32[256,1024]{0,1:T(8,128)} %copy-done.25, f32[256,1024]{0,1:T(8,128)} %get-tuple-element.44, f32[]{:T(128)S(6)} %div.152, f32[256,1024]{0,1:T(8,128)S(1)} %fusion.19, ...), kind=kLoop, calls=%fused_computation.53 | loop fusion | flops 3407872 | bytes 9437188 | tf_op jit(solution)/shard_map/div | solution.py:87
  80.4 4.5 %collective-permute-start.6 = (f32[1,1024]{0,1:T(8,128)S(1)}, f32[1,1024]{0,1:T(8,128)S(1)}, u32[]{:S(2)}, u32[]{:S(2)}) collective-permute-start(f32[1,1024]{0,1:T(8,128)S(1)} %slice.229), channel_id=1, source_target_pairs={{0,16},{16,32},{32,48},{48,64},{64,80},{80,96},{96,112},{1,17},{17... | collective-permute-start | bytes 12296 | tf_op jit(solution)/shard_map/ppermute | solution.py:47
  87.8 3.2 %collective-permute-done.6 = f32[1,1024]{0,1:T(8,128)S(1)} collective-permute-done((f32[1,1024]{0,1:T(8,128)S(1)}, f32[1,1024]{0,1:T(8,128)S(1)}, u32[]{:S(2)}, u32[]{:S(2)}) %collective-permute-start.6) | collective-permute-done | bytes 4128 | tf_op jit(solution)/shard_map/ppermute | solution.py:47
  91.0 2.6 %abs_reduce_fusion.6 = (f32[]{:T(128)}, f32[256,1024]{0,1:T(8,128)S(1)}, f32[256,1024]{0,1:T(8,128)}) fusion(f32[256,1024]{0,1:T(8,128)S(1)} %copy-done.31, f32[256,1024]{0,1:T(8,128)S(1)} %copy-done.5, f32[]{:T(128)} %bitcast.7, f32[256,1024]{0,1:T(8,128)S(1)} %copy.50, f32[256,1024]{0,1:T(8,128)S(1)} %copy-done.16, f32[256,1024]{0,1:T(8,128)S(1)} %get-tuple-element.37, ...), kind=kLoop, calls=%fused_computation.49 | loop fusion | flops 4718591 | bytes 10485768 | tf_op jit(solution)/shard_map/reduce_sum | solution.py:101
  97.9 8.8 %collective-permute-done.8 = f32[1,1024]{0,1:T(8,128)S(1)} collective-permute-done((f32[1,1024]{0,1:T(8,128)S(1)}, f32[1,1024]{0,1:T(8,128)S(1)}, u32[]{:S(2)}, u32[]{:S(2)}) %collective-permute-start.8) | collective-permute-done | bytes 4128 | tf_op jit(solution)/shard_map/ppermute | solution.py:47
  107.0 3.1 %abs_reduce_fusion.4 = (f32[]{:T(128)}, f32[256,1024]{0,1:T(8,128)}, f32[]{:T(128)}, f32[256,1024]{0,1:T(8,128)}) fusion(f32[256,1024]{0,1:T(8,128)S(1)} %copy-done.21, f32[256,1024]{0,1:T(8,128)S(1)} %copy-done.13, f32[256,1024]{0,1:T(8,128)S(1)} %get-tuple-element.37, f32[]{:T(128)S(6)} %div.152, f32[256,1024]{0,1:T(8,128)S(1)} %get-tuple-element.31, ...), kind=kLoop, calls=%fused_computation.47 | loop fusion | flops 4194302 | bytes 11534348 | tf_op jit(solution)/shard_map/reduce_sum | solution.py:102
  112.1 12.1 %all_to_all.50 = f32[32,1,2]{2,1,0:T(1,128)S(1)} all-to-all(f32[32,1,2]{2,1,0:T(1,128)S(1)} %broadcast_in_dim.26), channel_id=1, replica_groups=mesh['row_0'=4,'row_1'=2,'col_0'=4,'col_1'=4] {'row_1','col_0','col_1'}, dimensions={0} | all-to-all | bytes 512 | tf_op jit(solution)/shard_map/all_to_all | solution.py:21
  124.3 7.0 %all_to_all.51 = f32[4,1,2]{2,1,0:T(1,128)S(1)} all-to-all(f32[4,1,2]{2,1,0:T(1,128)S(1)} %broadcast_in_dim.27), channel_id=1, replica_groups=mesh['row_0'=4,'row_1'=2,'col_0'=4,'col_1'=4] {'row_0'}, dimensions={0} | all-to-all | bytes 64 | tf_op jit(solution)/shard_map/all_to_all | solution.py:21
  133.4 3.2 %fusion.14 = (f32[256,1024]{0,1:T(8,128)S(1)}, f32[256,1024]{0,1:T(8,128)S(1)}, f32[256,1024]{0,1:T(8,128)S(1)}) fusion(f32[256,1024]{0,1:T(8,128)} %copy-done.10, f32[256,1024]{0,1:T(8,128)} %get-tuple-element.44, f32[256,1024]{0,1:T(8,128)} %get-tuple-element.34, f32[]{:T(128)S(6)} %div.163, f32[256,1024]{0,1:T(8,128)S(1)} %fusion.17, ...), kind=kLoop, calls=%fused_computation.44 | loop fusion | flops 3407872 | bytes 9437188 | tf_op jit(solution)/shard_map/div | solution.py:87
  137.4 4.3 %collective-permute-start.10 = (f32[1,1024]{0,1:T(8,128)S(1)}, f32[1,1024]{0,1:T(8,128)S(1)}, u32[]{:S(2)}, u32[]{:S(2)}) collective-permute-start(f32[1,1024]{0,1:T(8,128)S(1)} %slice.239), channel_id=1, source_target_pairs={{0,16},{16,32},{32,48},{48,64},{64,80},{80,96},{96,112},{1,17},{17... | collective-permute-start | bytes 12296 | tf_op jit(solution)/shard_map/ppermute | solution.py:47
  144.6 3.2 %collective-permute-done.10 = f32[1,1024]{0,1:T(8,128)S(1)} collective-permute-done((f32[1,1024]{0,1:T(8,128)S(1)}, f32[1,1024]{0,1:T(8,128)S(1)}, u32[]{:S(2)}, u32[]{:S(2)}) %collective-permute-start.10) | collective-permute-done | bytes 4128 | tf_op jit(solution)/shard_map/ppermute | solution.py:47
  147.8 2.5 %abs_reduce_fusion.3 = (f32[]{:T(128)}, f32[256,1024]{0,1:T(8,128)S(1)}, f32[256,1024]{0,1:T(8,128)}) fusion(f32[256,1024]{0,1:T(8,128)S(1)} %copy-done.30, f32[256,1024]{0,1:T(8,128)S(1)} %copy-done.3, f32[]{:T(128)S(6)} %mul.172, f32[256,1024]{0,1:T(8,128)S(1)} %copy.50, f32[256,1024]{0,1:T(8,128)S(1)} %copy-done.17, ...), kind=kLoop, calls=%fused_computation.40 | loop fusion | flops 4718591 | bytes 10485768 | tf_op jit(solution)/shard_map/reduce_sum | solution.py:101
  154.7 9.0 %collective-permute-done.12 = f32[1,1024]{0,1:T(8,128)S(1)} collective-permute-done((f32[1,1024]{0,1:T(8,128)S(1)}, f32[1,1024]{0,1:T(8,128)S(1)}, u32[]{:S(2)}, u32[]{:S(2)}) %collective-permute-start.12) | collective-permute-done | bytes 4128 | tf_op jit(solution)/shard_map/ppermute | solution.py:47
  163.9 3.2 %abs_reduce_fusion.1 = (f32[]{:T(128)}, f32[256,1024]{0,1:T(8,128)}, f32[]{:T(128)}, f32[256,1024]{0,1:T(8,128)}) fusion(f32[256,1024]{0,1:T(8,128)S(1)} %copy-done.19, f32[256,1024]{0,1:T(8,128)S(1)} %copy-done.11, f32[256,1024]{0,1:T(8,128)S(1)} %get-tuple-element.27, f32[]{:T(128)S(6)} %div.163, f32[256,1024]{0,1:T(8,128)S(1)} %get-tuple-element.21, ...), kind=kLoop, calls=%fused_computation.38 | loop fusion | flops 4194302 | bytes 11534348 | tf_op jit(solution)/shard_map/reduce_sum | solution.py:102
  169.1 12.1 %all_to_all.52 = f32[32,1,2]{2,1,0:T(1,128)S(1)} all-to-all(f32[32,1,2]{2,1,0:T(1,128)S(1)} %broadcast_in_dim.28), channel_id=1, replica_groups=mesh['row_0'=4,'row_1'=2,'col_0'=4,'col_1'=4] {'row_1','col_0','col_1'}, dimensions={0} | all-to-all | bytes 512 | tf_op jit(solution)/shard_map/all_to_all | solution.py:21
  181.3 7.0 %all_to_all.53 = f32[4,1,2]{2,1,0:T(1,128)S(1)} all-to-all(f32[4,1,2]{2,1,0:T(1,128)S(1)} %broadcast_in_dim.29), channel_id=1, replica_groups=mesh['row_0'=4,'row_1'=2,'col_0'=4,'col_1'=4] {'row_0'}, dimensions={0} | all-to-all | bytes 64 | tf_op jit(solution)/shard_map/all_to_all | solution.py:21
  190.4 3.2 %fusion.12 = (f32[256,1024]{0,1:T(8,128)S(1)}, f32[256,1024]{0,1:T(8,128)S(1)}, f32[256,1024]{0,1:T(8,128)S(1)}) fusion(f32[256,1024]{0,1:T(8,128)} %copy-done.8, f32[256,1024]{0,1:T(8,128)} %get-tuple-element.34, f32[256,1024]{0,1:T(8,128)} %get-tuple-element.24, f32[]{:T(128)S(6)} %div.174, f32[256,1024]{0,1:T(8,128)S(1)} %fusion.15, ...), kind=kLoop, calls=%fused_computation.35 | loop fusion | flops 3407872 | bytes 9437188 | tf_op jit(solution)/shard_map/div | solution.py:87
  194.3 4.3 %collective-permute-start.14 = (f32[1,1024]{0,1:T(8,128)S(1)}, f32[1,1024]{0,1:T(8,128)S(1)}, u32[]{:S(2)}, u32[]{:S(2)}) collective-permute-start(f32[1,1024]{0,1:T(8,128)S(1)} %slice.249), channel_id=1, source_target_pairs={{0,16},{16,32},{32,48},{48,64},{64,80},{80,96},{96,112},{1,17},{17... | collective-permute-start | bytes 12296 | tf_op jit(solution)/shard_map/ppermute | solution.py:47
  201.5 3.2 %collective-permute-done.14 = f32[1,1024]{0,1:T(8,128)S(1)} collective-permute-done((f32[1,1024]{0,1:T(8,128)S(1)}, f32[1,1024]{0,1:T(8,128)S(1)}, u32[]{:S(2)}, u32[]{:S(2)}) %collective-permute-start.14) | collective-permute-done | bytes 4128 | tf_op jit(solution)/shard_map/ppermute | solution.py:47
  209.8 9.0 %collective-permute-done.16 = f32[1,1024]{0,1:T(8,128)S(1)} collective-permute-done((f32[1,1024]{0,1:T(8,128)S(1)}, f32[1,1024]{0,1:T(8,128)S(1)}, u32[]{:S(2)}, u32[]{:S(2)}) %collective-permute-start.16) | collective-permute-done | bytes 4128 | tf_op jit(solution)/shard_map/ppermute | solution.py:47
  223.1 5.5 %all-to-all-start.6 = ((f32[32,1,2]{2,1,0:T(1,128)}), f32[32,1,2]{2,1,0:T(1,128)S(1)}, u32[]{:S(2)}, u32[]{:S(2)}) async-start(f32[32,1,2]{2,1,0:T(1,128)} %broadcast_in_dim.30), calls=%async_computation.6 | async-start | bytes 32768 | tf_op jit(solution)/shard_map/all_to_all | solution.py:21
  235.3 7.0 %all_to_all.54 = f32[4,1,2]{2,1,0:T(1,128)S(1)} all-to-all(f32[4,1,2]{2,1,0:T(1,128)S(1)} %broadcast_in_dim.31), channel_id=1, replica_groups=mesh['row_0'=4,'row_1'=2,'col_0'=4,'col_1'=4] {'row_0'}, dimensions={0} | all-to-all | bytes 64 | tf_op jit(solution)/shard_map/all_to_all | solution.py:21
  (164 shorter events, 53.3 us)
Async XLA Ops:
  1.6 8.8 %collective-permute-start.1 = (f32[1,256]{1,0:T(1,128)S(1)}, f32[1,256]{1,0:T(1,128)S(1)}, u32[]{:S(2)}, u32[]{:S(2)}) collective-permute-start(f32[1,256]{1,0:T(1,128)S(1)} %bitcast.63), channel_id=1, source_target_pairs={{1,0},{2,1},{3,2},{4,3},{5,4},{6,5},{7,6},{8,7},{9,8},{10,9},{11,1... | collective-permute-start | bytes 3080 | tf_op jit(solution)/shard_map/ppermute | solution.py:47
  4.0 11.5 %collective-permute-start = (f32[1,1024]{0,1:T(8,128)S(1)}, f32[1,1024]{0,1:T(8,128)}, u32[]{:S(2)}, u32[]{:S(2)}) collective-permute-start(f32[1,1024]{0,1:T(8,128)S(1)} %copy.44), channel_id=1, source_target_pairs={{16,0},{32,16},{48,32},{64,48},{80,64},{96,80},{112,96},{17,1},{33... | collective-permute-start | bytes 12296 | tf_op jit(solution)/shard_map/ppermute | solution.py:47
  17.3 59.4 %copy-start.12 = (f32[256,1024]{0,1:T(8,128)}, f32[256,1024]{0,1:T(8,128)S(1)}, u32[]{:S(2)}) copy-start(f32[256,1024]{0,1:T(8,128)S(1)} %get-tuple-element.47) | copy-start | bytes 3145732
  19.2 8.7 %collective-permute-start.2 = (f32[1,1024]{0,1:T(8,128)}, f32[1,1024]{0,1:T(8,128)}, u32[]{:S(2)}, u32[]{:S(2)}) collective-permute-start(f32[1,1024]{0,1:T(8,128)} %slice.219), channel_id=1, source_target_pairs={{0,16},{16,32},{32,48},{48,64},{64,80},{80,96},{96,112},{1,17},{17... | collective-permute-start | bytes 12296 | tf_op jit(solution)/shard_map/ppermute | solution.py:47
  21.1 6.8 %collective-permute-start.3 = (f32[1,256]{1,0:T(1,128)S(1)}, f32[1,256]{1,0:T(1,128)S(1)}, u32[]{:S(2)}, u32[]{:S(2)}) collective-permute-start(f32[1,256]{1,0:T(1,128)S(1)} %slice_bitcast_fusion.7), channel_id=1, source_target_pairs={{0,1},{1,2},{2,3},{3,4},{4,5},{5,6},{6,7},{7,8},{8,9},{9,10},{10,1... | collective-permute-start | bytes 3080 | tf_op jit(solution)/shard_map/ppermute | solution.py:47
  31.5 12.9 %copy-start.4 = (f32[256,1024]{0,1:T(8,128)}, f32[256,1024]{0,1:T(8,128)S(1)}, u32[]{:S(2)}) copy-start(f32[256,1024]{0,1:T(8,128)S(1)} %get-tuple-element.41) | copy-start | bytes 3145732
  31.5 5.4 %collective-permute-start.5 = (f32[1,256]{1,0:T(1,128)S(1)}, f32[1,256]{1,0:T(1,128)S(1)}, u32[]{:S(2)}, u32[]{:S(2)}) collective-permute-start(f32[1,256]{1,0:T(1,128)S(1)} %slice_bitcast_fusion.6), channel_id=1, source_target_pairs={{1,0},{2,1},{3,2},{4,3},{5,4},{6,5},{7,6},{8,7},{9,8},{10,9},{11,1... | collective-permute-start | bytes 3080 | tf_op jit(solution)/shard_map/ppermute | solution.py:47
  33.3 11.0 %collective-permute-start.4 = (f32[1,1024]{0,1:T(8,128)S(1)}, f32[1,1024]{0,1:T(8,128)S(1)}, u32[]{:S(2)}, u32[]{:S(2)}) collective-permute-start(f32[1,1024]{0,1:T(8,128)S(1)} %slice.225), channel_id=1, source_target_pairs={{16,0},{32,16},{48,32},{64,48},{80,64},{96,80},{112,96},{17,1},{33... | collective-permute-start | bytes 12296 | tf_op jit(solution)/shard_map/ppermute | solution.py:47
  79.7 27.3 %copy-start.10 = (f32[256,1024]{0,1:T(8,128)}, f32[256,1024]{0,1:T(8,128)S(1)}, u32[]{:S(2)}) copy-start(f32[256,1024]{0,1:T(8,128)S(1)} %get-tuple-element.37) | copy-start | bytes 3145732
  80.2 53.2 %copy-start = (f32[256,1024]{0,1:T(8,128)}, f32[256,1024]{0,1:T(8,128)S(1)}, u32[]{:S(2)}) copy-start(f32[256,1024]{0,1:T(8,128)S(1)} %fusion.17) | copy-start | bytes 3145732
  80.4 10.6 %collective-permute-start.6 = (f32[1,1024]{0,1:T(8,128)S(1)}, f32[1,1024]{0,1:T(8,128)S(1)}, u32[]{:S(2)}, u32[]{:S(2)}) collective-permute-start(f32[1,1024]{0,1:T(8,128)S(1)} %slice.229), channel_id=1, source_target_pairs={{0,16},{16,32},{32,48},{48,64},{64,80},{80,96},{96,112},{1,17},{17... | collective-permute-start | bytes 12296 | tf_op jit(solution)/shard_map/ppermute | solution.py:47
  84.9 2.9 %collective-permute-start.7 = (f32[1,256]{1,0:T(1,128)S(1)}, f32[1,256]{1,0:T(1,128)S(1)}, u32[]{:S(2)}, u32[]{:S(2)}) collective-permute-start(f32[1,256]{1,0:T(1,128)S(1)} %slice_bitcast_fusion.5), channel_id=1, source_target_pairs={{0,1},{1,2},{2,3},{3,4},{4,5},{5,6},{6,7},{7,8},{8,9},{9,10},{10,1... | collective-permute-start | bytes 3080 | tf_op jit(solution)/shard_map/ppermute | solution.py:47
  93.6 13.4 %copy-start.2 = (f32[256,1024]{0,1:T(8,128)}, f32[256,1024]{0,1:T(8,128)S(1)}, u32[]{:S(2)}) copy-start(f32[256,1024]{0,1:T(8,128)S(1)} %get-tuple-element.31) | copy-start | bytes 3145732
  93.6 4.3 %collective-permute-start.9 = (f32[1,256]{1,0:T(1,128)S(1)}, f32[1,256]{1,0:T(1,128)S(1)}, u32[]{:S(2)}, u32[]{:S(2)}) collective-permute-start(f32[1,256]{1,0:T(1,128)S(1)} %slice_bitcast_fusion.4), channel_id=1, source_target_pairs={{1,0},{2,1},{3,2},{4,3},{5,4},{6,5},{7,6},{8,7},{9,8},{10,9},{11,1... | collective-permute-start | bytes 3080 | tf_op jit(solution)/shard_map/ppermute | solution.py:47
  95.4 11.4 %collective-permute-start.8 = (f32[1,1024]{0,1:T(8,128)S(1)}, f32[1,1024]{0,1:T(8,128)S(1)}, u32[]{:S(2)}, u32[]{:S(2)}) collective-permute-start(f32[1,1024]{0,1:T(8,128)S(1)} %slice.235), channel_id=1, source_target_pairs={{16,0},{32,16},{48,32},{64,48},{80,64},{96,80},{112,96},{17,1},{33... | collective-permute-start | bytes 12296 | tf_op jit(solution)/shard_map/ppermute | solution.py:47
  136.7 27.2 %copy-start.8 = (f32[256,1024]{0,1:T(8,128)}, f32[256,1024]{0,1:T(8,128)S(1)}, u32[]{:S(2)}) copy-start(f32[256,1024]{0,1:T(8,128)S(1)} %get-tuple-element.27) | copy-start | bytes 3145732
  137.4 10.5 %collective-permute-start.10 = (f32[1,1024]{0,1:T(8,128)S(1)}, f32[1,1024]{0,1:T(8,128)S(1)}, u32[]{:S(2)}, u32[]{:S(2)}) collective-permute-start(f32[1,1024]{0,1:T(8,128)S(1)} %slice.239), channel_id=1, source_target_pairs={{0,16},{16,32},{32,48},{48,64},{64,80},{80,96},{96,112},{1,17},{17... | collective-permute-start | bytes 12296 | tf_op jit(solution)/shard_map/ppermute | solution.py:47
  141.7 2.9 %collective-permute-start.11 = (f32[1,256]{1,0:T(1,128)S(1)}, f32[1,256]{1,0:T(1,128)S(1)}, u32[]{:S(2)}, u32[]{:S(2)}) collective-permute-start(f32[1,256]{1,0:T(1,128)S(1)} %slice_bitcast_fusion.3), channel_id=1, source_target_pairs={{0,1},{1,2},{2,3},{3,4},{4,5},{5,6},{6,7},{7,8},{8,9},{9,10},{10,1... | collective-permute-start | bytes 3080 | tf_op jit(solution)/shard_map/ppermute | solution.py:47
  150.4 4.3 %collective-permute-start.13 = (f32[1,256]{1,0:T(1,128)S(1)}, f32[1,256]{1,0:T(1,128)S(1)}, u32[]{:S(2)}, u32[]{:S(2)}) collective-permute-start(f32[1,256]{1,0:T(1,128)S(1)} %slice_bitcast_fusion.2), channel_id=1, source_target_pairs={{1,0},{2,1},{3,2},{4,3},{5,4},{6,5},{7,6},{8,7},{9,8},{10,9},{11,1... | collective-permute-start | bytes 3080 | tf_op jit(solution)/shard_map/ppermute | solution.py:47
  151.7 12.2 %copy-start.20 = (f32[256,1024]{0,1:T(8,128)S(1)}, f32[256,1024]{0,1:T(8,128)}, u32[]{:S(2)}) copy-start(f32[256,1024]{0,1:T(8,128)} %get-tuple-element.53) | copy-start | bytes 3145732
  152.2 11.5 %collective-permute-start.12 = (f32[1,1024]{0,1:T(8,128)S(1)}, f32[1,1024]{0,1:T(8,128)S(1)}, u32[]{:S(2)}, u32[]{:S(2)}) collective-permute-start(f32[1,1024]{0,1:T(8,128)S(1)} %slice.245), channel_id=1, source_target_pairs={{16,0},{32,16},{48,32},{64,48},{80,64},{96,80},{112,96},{17,1},{33... | collective-permute-start | bytes 12296 | tf_op jit(solution)/shard_map/ppermute | solution.py:47
  193.6 25.4 %copy-start.15 = (f32[256,1024]{0,1:T(8,128)}, f32[256,1024]{0,1:T(8,128)S(1)}, u32[]{:S(2)}) copy-start(f32[256,1024]{0,1:T(8,128)S(1)} %get-tuple-element.17) | copy-start | bytes 3145732
  194.1 24.9 %copy-start.14 = (f32[256,1024]{0,1:T(8,128)}, f32[256,1024]{0,1:T(8,128)S(1)}, u32[]{:S(2)}) copy-start(f32[256,1024]{0,1:T(8,128)S(1)} %fusion.13) | copy-start | bytes 3145732
  194.3 10.5 %collective-permute-start.14 = (f32[1,1024]{0,1:T(8,128)S(1)}, f32[1,1024]{0,1:T(8,128)S(1)}, u32[]{:S(2)}, u32[]{:S(2)}) collective-permute-start(f32[1,1024]{0,1:T(8,128)S(1)} %slice.249), channel_id=1, source_target_pairs={{0,16},{16,32},{32,48},{48,64},{64,80},{80,96},{96,112},{1,17},{17... | collective-permute-start | bytes 12296 | tf_op jit(solution)/shard_map/ppermute | solution.py:47
  198.6 2.9 %collective-permute-start.15 = (f32[1,256]{1,0:T(1,128)S(1)}, f32[1,256]{1,0:T(1,128)S(1)}, u32[]{:S(2)}, u32[]{:S(2)}) collective-permute-start(f32[1,256]{1,0:T(1,128)S(1)} %slice_bitcast_fusion.1), channel_id=1, source_target_pairs={{0,1},{1,2},{2,3},{3,4},{4,5},{5,6},{6,7},{7,8},{8,9},{9,10},{10,1... | collective-permute-start | bytes 3080 | tf_op jit(solution)/shard_map/ppermute | solution.py:47
  205.4 13.6 %copy-start.6 = (f32[256,1024]{0,1:T(8,128)}, f32[256,1024]{0,1:T(8,128)S(1)}, u32[]{:S(2)}) copy-start(f32[256,1024]{0,1:T(8,128)S(1)} %get-tuple-element.15) | copy-start | bytes 3145732
  205.4 4.3 %collective-permute-start.17 = (f32[1,256]{1,0:T(1,128)S(1)}, f32[1,256]{1,0:T(1,128)S(1)}, u32[]{:S(2)}, u32[]{:S(2)}) collective-permute-start(f32[1,256]{1,0:T(1,128)S(1)} %slice_bitcast_fusion), channel_id=1, source_target_pairs={{1,0},{2,1},{3,2},{4,3},{5,4},{6,5},{7,6},{8,7},{9,8},{10,9},{11,1... | collective-permute-start | bytes 3080 | tf_op jit(solution)/shard_map/ppermute | solution.py:47
  206.8 12.2 %copy-start.29 = (f32[256,1024]{0,1:T(8,128)S(1)}, f32[256,1024]{0,1:T(8,128)}, u32[]{:S(2)}) copy-start(f32[256,1024]{0,1:T(8,128)} %get-tuple-element.22) | copy-start | bytes 3145732
  206.9 12.1 %copy-start.9 = (f32[256,1024]{0,1:T(8,128)S(1)}, f32[256,1024]{0,1:T(8,128)}, u32[]{:S(2)}) copy-start(f32[256,1024]{0,1:T(8,128)} %copy-done.8) | copy-start | bytes 3145732
  206.9 12.1 %copy-start.27 = (f32[256,1024]{0,1:T(8,128)S(1)}, f32[256,1024]{0,1:T(8,128)}, u32[]{:S(2)}) copy-start(f32[256,1024]{0,1:T(8,128)} %get-tuple-element.24) | copy-start | bytes 3145732
  207.2 11.5 %collective-permute-start.16 = (f32[1,1024]{0,1:T(8,128)S(1)}, f32[1,1024]{0,1:T(8,128)S(1)}, u32[]{:S(2)}, u32[]{:S(2)}) collective-permute-start(f32[1,1024]{0,1:T(8,128)S(1)} %slice.255), channel_id=1, source_target_pairs={{16,0},{32,16},{48,32},{64,48},{80,64},{96,80},{112,96},{17,1},{33... | collective-permute-start | bytes 12296 | tf_op jit(solution)/shard_map/ppermute | solution.py:47
  223.1 12.2 %all-to-all-start.6 = ((f32[32,1,2]{2,1,0:T(1,128)}), f32[32,1,2]{2,1,0:T(1,128)S(1)}, u32[]{:S(2)}, u32[]{:S(2)}) async-start(f32[32,1,2]{2,1,0:T(1,128)} %broadcast_in_dim.30), calls=%async_computation.6 | async-start | bytes 32768 | tf_op jit(solution)/shard_map/all_to_all | solution.py:21
  (20 other events, 197.6 us)
where the time goes:
time: 248 us; the launch traced here: 245 us
  blocking collectives  70.6 us (28%)
  waiting for transfers between devices  53.9 us (22%)
  starting transfers between devices  51.1 us (21%)
  other arithmetic  38.7 us (16%)
  local copies, waits for them, and re-layouts  17.7 us (7%)
  between operations  13.3 us (5%)
    all_to_all x7, blocking collectives, sent_to_all(): return lax.all_to_all(copies, axis, split_axis=0, concat_axis=0, tiled=True)  70.6 us
    ppermute x18, waiting for transfers between devices, passed_along(): lax.ppermute(value, axis, [(source, source + steps) for source in range(i...  52 us
    ppermute x18, starting transfers between devices, passed_along(): lax.ppermute(value, axis, [(source, source + steps) for source in range(i...  45.6 us
    reduce_sum x4, other arithmetic, on_device(): primal_part = jnp.sum(jnp.abs(change / tau + div_prev - div_new))  10.3 us
    div x4, other arithmetic, on_device(): new_y = moved_y / shrink  10 us
    reduce_sum x3, other arithmetic, on_device(): jnp.sum(jnp.abs((dual_y - new_y) / sigma - change_y))  9.05 us
    unnamed x70, local copies, waits for them, and re-layouts  7.37 us
    all_to_all x1, starting transfers between devices, sent_to_all(): return lax.all_to_all(copies, axis, split_axis=0, concat_axis=0, tiled=True)  5.46 us
  transfers between devices with their start and end apart: 19, of which 15 were waited for; matrix products, arithmetic and copies ran while one was open for 5% of the time, Pallas kernels for 0%

commit v1 on v0

v1 whole, which is shorter than its diff:
```python
import functools
import jax
import jax.numpy as jnp
import numpy as np
from jax import lax
from jax.experimental import pallas as pl
from jax.experimental.pallas import tpu as pltpu
from jax.sharding import PartitionSpec as P

ITERS = 4
MESH = pl.DeviceIdType.MESH

first_tau = np.float32(0.35)
step_product = np.float32(0.124)
adapt_rate = 0.5
adapt_decay = 0.9
epsilon = np.float32(1e-06)

SUB = 8
LANE = 128
UNROLL = 3


def kernel(
    n_row, n_col, cells,
    noisy_hbm, fid_hbm,
    u_out, dual_out, tau_out,
    U, F, FN, UB, PX, PY, GX, GY, DV, QT, CB, rb1, rb2,
    load_sem, halo_send, halo_recv, red_send, red_recv,
):
    rows, cols = noisy_hbm.shape
    strips = rows // SUB + 2
    tiles = cols // LANE
    my_row, my_col = lax.axis_index("row"), lax.axis_index("col")
    f32 = jnp.float32

    def row_at(d):
        return lax.rem(my_row + d + n_row, n_row)

    def col_at(d):
        return lax.rem(my_col + d + n_col, n_col)

    sub = lax.broadcasted_iota(jnp.int32, (SUB, LANE), 0)
    lane = lax.broadcasted_iota(jnp.int32, (SUB, LANE), 1)
    sub_first, sub_last = sub == 0, sub == SUB - 1
    lane_first, lane_last = lane == 0, lane == LANE - 1

    CB[...] = jnp.zeros_like(CB)

    loads = [
        pltpu.make_async_copy(src, dst.at[SUB : SUB + rows, 0:cols], load_sem.at[i])
        for i, (src, dst) in enumerate(((noisy_hbm, U), (fid_hbm, F)))
    ]
    for load in loads:
        load.start()
    barrier = pltpu.get_barrier_semaphore()
    partners = [(row_at(d), my_col) for d in range(1, n_row)]
    partners += [(my_row, col_at(d)) for d in range(1, n_col)]
    partners += [(row_at(a), col_at(b)) for a in (-1, 1) for b in (-1, 1)]
    for partner in partners:
        pl.semaphore_signal(barrier, inc=1, device_id=partner, device_id_type=MESH)
    for load in loads:
        load.wait()

    def pack(b):
        at = pl.ds(SUB + b * LANE, LANE)
        lanes = lax.broadcasted_iota(jnp.int32, (LANE, LANE), 1)
        n0, n7 = U[at, 0:LANE], U[at, cols - LANE : cols]
        f0 = pltpu.roll(F[at, 0:LANE], 8, axis=1)
        f7 = pltpu.roll(F[at, cols - LANE : cols], LANE - 8, axis=1)
        low = jnp.where(lanes < 8, n0, f0)
        high = jnp.where(lanes >= LANE - 8, n7, f7)
        return jnp.where(lanes < LANE // 2, low, high).T

    for b in range(rows // LANE):
        QT[:, b * LANE : (b + 1) * LANE] = pack(b)

    pl.semaphore_wait(barrier, len(partners))

    low, high = slice(0, 16), slice(LANE - 16, LANE)
    mid = slice(LANE, LANE + rows)
    top, bottom = slice(0, LANE), slice(LANE + rows, 2 * LANE + rows)
    first, last = slice(0, LANE), slice(rows - LANE, rows)
    below_rows = slice(rows + SUB, rows + 2 * SUB)
    moves = []
    for src, dst in ((noisy_hbm, U), (fid_hbm, F)):
        moves.append((src.at[0:SUB, :], dst.at[below_rows, 0:cols], -1, 0))
        moves.append((src.at[rows - SUB : rows, :], dst.at[0:SUB, 0:cols], 1, 0))
    moves.append((QT.at[low, :], CB.at[low, mid], 0, -1))
    moves.append((QT.at[high, :], CB.at[high, mid], 0, 1))
    for side, step in ((low, -1), (high, 1)):
        moves.append((QT.at[side, last], CB.at[side, top], 1, step))
        moves.append((QT.at[side, first], CB.at[side, bottom], -1, step))
    halos = [
        pltpu.make_async_remote_copy(
            src_ref=src, dst_ref=dst, send_sem=halo_send.at[i], recv_sem=halo_recv.at[i],
            device_id=(row_at(a), col_at(b)), device_id_type=MESH,
        )
        for i, (src, dst, a, b) in enumerate(moves)
    ]
    for halo in halos:
        halo.start()
    for halo in halos:
        halo.wait_recv()

    def unpack(block, start, count, to):
        turned = block.T[start : start + count, :]
        lanes = lax.broadcasted_iota(jnp.int32, turned.shape, 1)
        edge = jnp.logical_or(lanes < 8, lanes >= LANE - 8)
        fid = jnp.where(
            lanes < LANE // 2, pltpu.roll(turned, LANE - 8, axis=1), pltpu.roll(turned, 8, axis=1)
        )
        U[to : to + count, cols : cols + LANE] = jnp.where(edge, turned, 0.0)
        F[to : to + count, cols : cols + LANE] = jnp.where(edge, fid, 1.0)

    unpack(CB[:, top], LANE - SUB, SUB, 0)
    for b in range(rows // LANE):
        unpack(CB[:, (b + 1) * LANE : (b + 2) * LANE], 0, LANE, SUB + b * LANE)
    unpack(CB[:, bottom], 0, SUB, SUB + rows)

    def at(s, c):
        start = s * SUB if isinstance(s, int) else pl.multiple_of(s * SUB, SUB)
        return pl.ds(start, SUB), slice(c * LANE, (c + 1) * LANE)

    at_left, at_right = my_col == 0, my_col == n_col - 1
    last_col = jnp.logical_and(at_right, lane_last)
    outside = jnp.logical_and(at_left, lane >= LANE // 2)
    in_first_row = jnp.logical_and(my_row == 0, sub_first)

    def gradient(field, extra):
        def body(s, carry):
            cell = my_row * rows + (s - 1) * SUB + sub
            inside = jnp.logical_and(cell >= 0, cell < n_row * rows - 1)
            after = jnp.minimum(s + 1, strips - 1)
            here = [field[at(s, c)] for c in range(tiles + 1)]
            turned = [pltpu.roll(h, LANE - 1, axis=1) for h in here]
            for c in range(tiles + 1):
                below = jnp.where(
                    sub_last,
                    pltpu.roll(field[at(after, c)], SUB - 1, axis=0),
                    pltpu.roll(here[c], SUB - 1, axis=0),
                )
                right = jnp.where(lane_last, turned[(c + 1) % (tiles + 1)], turned[c])
                gx = jnp.where(inside, below - here[c], 0.0)
                gy = right - here[c]
                if c == tiles - 1:
                    gy = jnp.where(last_col, 0.0, gy)
                if c == tiles:
                    gy = jnp.where(outside, 0.0, gy)
                GX[at(s, c)] = gx
                GY[at(s, c)] = gy
                if extra:
                    FN[at(s, c)] = F[at(s, c)] * here[c]
            return carry

        lax.fori_loop(0, strips, body, 0)

    gradient(U, True)

    def strip(k, s, carry, counted, tau, sigma, itau, isigma):
        prev_x, prev_w, acc_p, acc_d, acc_l = carry
        prev_x, prev_w = list(prev_x), list(prev_w)
        final = k == ITERS - 1
        first_strip = isinstance(s, int) and s == 1

        def dual_step(c):
            qx, qy = sigma * GX[at(s, c)], sigma * GY[at(s, c)]
            if k:
                px, py = PX[at(s, c)], PY[at(s, c)]
                qx, qy = px + qx, py + qy
            scale = lax.rsqrt(jnp.maximum(qx * qx + qy * qy, 1.0))
            nx, ny = qx * scale, qy * scale
            tx, ty = ((px - nx) * isigma, (py - ny) * isigma) if k else (-nx * isigma, -ny * isigma)
            return nx, ny, tx, ty, pltpu.roll(nx, 1, axis=0), pltpu.roll(ny, 1, axis=1)

        def primal_step(c, dual, left):
            nx, ny, tx, ty, rx, ry = dual
            div = (nx - jnp.where(sub_first, prev_x[c], rx)) + (ny - jnp.where(lane_first, left, ry))
            prev_x[c] = rx
            old = U[at(s, c)]
            new = (old + tau * (div + FN[at(s, c)])) / (1.0 + tau * F[at(s, c)])
            du = old - new
            wx, wy = tx + du, ty + du
            before = DV[at(s, c)] if k and counted and c < tiles else None
            if not final:
                PX[at(s, c)] = nx
                PY[at(s, c)] = ny
                U[at(s, c)] = new
                UB[at(s, c)] = 2.0 * new - old
                DV[at(s, c)] = div
            elif counted and c < tiles:
                own = at(s - 1, c)
                u_out[own] = new
                dual_out[(0, *own)] = nx
                dual_out[(1, *own)] = ny
            rwx, rwy = pltpu.roll(wx, 1, axis=0), pltpu.roll(wy, 1, axis=1)
            upper = prev_w[c]
            prev_w[c] = rwx
            return div, du, before, upper, rwx, rwy

        def residual(got, left):
            div, du, before, upper, rwx, rwy = got
            primal = du * itau - div
            if before is not None:
                primal = primal + before
            return (
                jnp.abs(primal),
                jnp.abs(jnp.where(sub_first, upper, rwx) - du),
                jnp.abs(jnp.where(lane_first, left, rwy) - du),
            )

        before_last = dual_step(tiles - 1)
        halo = dual_step(tiles)
        halo_got = primal_step(tiles, halo, before_last[5])
        left, left_w = halo[5], halo_got[5]
        for c in range(tiles):
            dual = before_last if c == tiles - 1 else dual_step(c)
            got = primal_step(c, dual, left)
            if counted:
                primal, along, across = residual(got, left_w)
                if first_strip:
                    along = jnp.where(in_first_row, 0.0, along)
                acc_p = acc_p + primal
                if c == 0:
                    acc_l = acc_l + across
                    acc_d = acc_d + along
                else:
                    acc_d = acc_d + (along + across)
            left, left_w = dual[5], got[5]
        return tuple(prev_x), tuple(prev_w), acc_p, acc_d, acc_l

    def reduce_start(k, primal, dual):
        rb1[k, my_row, 0:1, :] = jnp.sum(primal, axis=0, keepdims=True)
        rb1[k, my_row, 1:2, :] = jnp.sum(dual, axis=0, keepdims=True)
        for d in range(1, n_row):
            pltpu.make_async_remote_copy(
                src_ref=rb1.at[k, my_row], dst_ref=rb1.at[k, my_row],
                send_sem=red_send.at[k, 0], recv_sem=red_recv.at[k, 0],
                device_id=(row_at(d), my_col), device_id_type=MESH,
            ).start()

    def reduce_middle(k):
        got = rb1.at[k, 0 : n_row - 1]
        pltpu.make_async_copy(got, got, red_recv.at[k, 0]).wait()
        total = rb1[k, 0]
        for i in range(1, n_row):
            total = total + rb1[k, i]
        rb2[k, my_col] = total
        for d in range(1, n_col):
            pltpu.make_async_remote_copy(
                src_ref=rb2.at[k, my_col], dst_ref=rb2.at[k, my_col],
                send_sem=red_send.at[k, 1], recv_sem=red_recv.at[k, 1],
                device_id=(my_row, col_at(d)), device_id_type=MESH,
            ).start()

    def reduce_end(k):
        got = rb2.at[k, 0 : n_col - 1]
        pltpu.make_async_copy(got, got, red_recv.at[k, 1]).wait()
        total = rb2[k, 0]
        for i in range(1, n_col):
            total = total + rb2[k, i]
        total = jnp.sum(total, axis=1, keepdims=True)
        return total[0:1], total[1:2]

    zero = jnp.zeros((SUB, LANE), f32)
    tau_one = jnp.full((1, 1), first_tau, f32)
    sigma_one = jnp.full((1, 1), step_product / first_tau, f32)
    for k in range(ITERS):
        def full(x):
            return jnp.broadcast_to(x, (SUB, LANE))

        steps = (full(tau_one), full(sigma_one), full(1.0 / tau_one), full(1.0 / sigma_one))
        none = (zero,) * (tiles + 1)
        carry = strip(k, 0, (none, none, zero, zero, zero), False, *steps)
        carry = strip(k, 1, carry, True, *steps)

        def body(i, carry, k=k, steps=steps):
            for j in range(UNROLL):
                carry = strip(k, 2 + i * UNROLL + j, carry, True, *steps)
            return carry

        whole = (strips - 3) // UNROLL
        carry = lax.fori_loop(0, whole, body, carry)
        for s in range(2 + whole * UNROLL, strips - 1):
            carry = strip(k, s, carry, True, *steps)
        if k < ITERS - 1:
            carry = strip(k, strips - 1, carry, False, *steps)
        _, _, primal, dual, at_first = carry
        dual = dual + jnp.where(jnp.logical_and(at_left, lane_first), 0.0, at_first)
        reduce_start(k, primal, dual)
        reduce_middle(k)
        if k < ITERS - 1:
            gradient(UB, False)
        primal, dual = reduce_end(k)
        ratio = jnp.log((primal / cells + epsilon) / (dual / cells + epsilon))
        rate = np.float32(adapt_rate * adapt_decay**k)
        tau_one = tau_one * jnp.exp(rate * ratio / (1.0 + jnp.abs(ratio)))
        sigma_one = step_product / tau_one
    tau_out[...] = jnp.broadcast_to(tau_one, tau_out.shape)

    for halo in halos:
        halo.wait_send()
    for k in range(ITERS):
        sent = rb1.at[k, 0 : n_row - 1]
        pltpu.make_async_copy(sent, sent, red_send.at[k, 0]).wait()
        sent = rb2.at[k, 0 : n_col - 1]
        pltpu.make_async_copy(sent, sent, red_send.at[k, 1]).wait()


def solution(mesh):
    n_row, n_col = mesh.shape["row"], mesh.shape["col"]

    def on_device(noisy, fidelity):
        rows, cols = noisy.shape
        f32 = jnp.float32
        padded = pltpu.VMEM((rows + 2 * SUB, cols + LANE), f32)
        cells = np.float32(rows * cols * n_row * n_col)
        vmem = pl.BlockSpec(memory_space=pltpu.VMEM)
        current, dual, tau = pl.pallas_call(
            functools.partial(kernel, n_row, n_col, cells),
            out_shape=(
                jax.ShapeDtypeStruct((rows, cols), f32),
                jax.ShapeDtypeStruct((2, rows, cols), f32),
                jax.ShapeDtypeStruct((1, LANE), f32),
            ),
            in_specs=[pl.BlockSpec(memory_space=pl.ANY)] * 2,
            out_specs=(vmem, vmem, vmem),
            scratch_shapes=[padded] * 9
            + [
                pltpu.VMEM((LANE, rows), f32),
                pltpu.VMEM((LANE, rows + 2 * LANE), f32),
                pltpu.VMEM((ITERS, n_row, 2, LANE), f32),
                pltpu.VMEM((ITERS, n_col, 2, LANE), f32),
                pltpu.SemaphoreType.DMA((2,)),
                pltpu.SemaphoreType.DMA((10,)),
                pltpu.SemaphoreType.DMA((10,)),
                pltpu.SemaphoreType.DMA((ITERS, 2)),
                pltpu.SemaphoreType.DMA((ITERS, 2)),
            ],
            compiler_params=pltpu.CompilerParams(
                collective_id=0, has_side_effects=True, vmem_limit_bytes=40 * 1024 * 1024
            ),
        )(noisy, fidelity)
        return current, dual, tau[0, 0]

    return jax.shard_map(
        on_device,
        mesh=mesh,
        in_specs=(P("row", "col"), P("row", "col")),
        out_specs=(P("row", "col"), P(None, "row", "col"), P()),
        check_vma=False,
    )
```

time: 248 us -> 65.9 us (0.27)
  blocking collectives: 70.6 us -> 0 us
  Pallas kernels: 0 us -> 59.1 us
  waiting for transfers between devices: 53.9 us -> 0 us
  starting transfers between devices: 51.1 us -> 0 us
  other arithmetic: 38.7 us -> 0 us
  local copies, waits for them, and re-layouts: 17.7 us -> 4.73 us
  between operations: 13.3 us -> 1.81 us
    all_to_all x7 -> x0, blocking collectives: 70.6 us -> none  [sent_to_all(): return lax.all_to_all(copies, axis, split_axis=0, concat_axis=0, tiled=True)]
    pallas_call x0 -> x1, Pallas kernels: none -> 59.1 us  [on_device(): pl.pallas_call(functools.partial(kernel, n_row, n_col, cells), out_shape=...]
    ppermute x18 -> x0, waiting for transfers between devices: 52 us -> none  [passed_along(): lax.ppermute(value, axis, [(source, source + steps) for source in range(i...]
    ppermute x18 -> x0, starting transfers between devices: 45.6 us -> none  [passed_along(): lax.ppermute(value, axis, [(source, source + steps) for source in range(i...]
    reduce_sum x15 -> x0, other arithmetic: 19.6 us -> none  [the longest x4 10.3 us: on_device(): primal_part = jnp.sum(jnp.abs(change / tau + div_prev - div_new))]
    div x9 -> x0, other arithmetic: 12.6 us -> none  [the longest x4 10 us: on_device(): new_y = moved_y / shrink]
    slice x26 -> x0, local copies, waits for them, and re-layouts: 9.67 us -> none  [the longest x5 2.65 us: diff_rows(): return jnp.concatenate([field[..., 1:, :], below], axis=-2) - field]
    all_to_all x1 -> x0, starting transfers between devices: 5.46 us -> none  [sent_to_all(): return lax.all_to_all(copies, axis, split_axis=0, concat_axis=0, tiled=True)]
  transfers between devices with their start and end apart: 19 -> 0, of which waited for: 15 -> 0; matrix products, arithmetic and copies ran while one was open for 5% -> 0% of each run, Pallas kernels for 0% -> 0%
where the time goes in v1:
time: 65.9 us; the launch traced here: 65.7 us
  Pallas kernels  59.1 us (90%)
  local copies, waits for them, and re-layouts  4.73 us (7%)
  between operations  1.81 us (3%)
    pallas_call x1, Pallas kernels, on_device(): pl.pallas_call(functools.partial(kernel, n_row, n_col, cells), out_shape=...  59.1 us
    unnamed x6, local copies, waits for them, and re-layouts  4.73 us

profile of v1, /device:TPU:1, one launch (start us, length us, event | category | flops | bytes accessed | tf_op | source)
XLA Modules:
  0.0 65.7 jit_solution(557495635640416820)
XLA Ops:
  0.6 0.0 copy-start
  0.6 1.2 %copy-done = f32[256,1024]{1,0:T(8,128)S(1)} copy-done((f32[256,1024]{1,0:T(8,128)S(1)}, f32[256,1024]{1,0:T(8,128)}, u32[]{:S(2)}) %copy-start) | copy-done | bytes 1048600
  1.9 0.0 copy-start.1
  1.9 1.2 %copy-done.1 = f32[256,1024]{1,0:T(8,128)S(1)} copy-done((f32[256,1024]{1,0:T(8,128)S(1)}, f32[256,1024]{1,0:T(8,128)}, u32[]{:S(2)}) %copy-start.1) | copy-done | bytes 1048600
  3.1 59.1 %shard_map.49 = (f32[256,1024]{1,0:T(8,128)S(1)}, f32[2,256,1024]{2,1,0:T(8,128)S(1)}, f32[1,128]{1,0:T(1,128)S(1)}) custom-call(f32[256,1024]{1,0:T(8,128)S(1)} %copy-done, f32[256,1024]{1,0:T(8,128)S(1)} %copy-done.1), custom_call_target="tpu_custom_call" | custom-call | tf_op jit(solution)/shard_map/pallas_call | solution.py:319
  62.2 1.0 %copy.8 = f32[256,1024]{1,0:T(8,128)} copy(f32[256,1024]{1,0:T(8,128)S(1)} %get-tuple-element.12) | data formatting | bytes 2097152
  63.2 1.3 %copy.9 = f32[2,256,1024]{2,1,0:T(8,128)} copy(f32[2,256,1024]{2,1,0:T(8,128)S(1)} %get-tuple-element.13) | data formatting | bytes 4194304
Async XLA Ops:
  0.6 1.2 %copy-start = (f32[256,1024]{1,0:T(8,128)S(1)}, f32[256,1024]{1,0:T(8,128)}, u32[]{:S(2)}) copy-start(f32[256,1024]{1,0:T(8,128)} %noisy_hbm.1) | copy-start | bytes 3145732
  1.9 1.2 %copy-start.1 = (f32[256,1024]{1,0:T(8,128)S(1)}, f32[256,1024]{1,0:T(8,128)}, u32[]{:S(2)}) copy-start(f32[256,1024]{1,0:T(8,128)} %fid_hbm.1) | copy-start | bytes 3145732

commit v2 on v1

v2 whole, which is shorter than its diff:
```python
import functools
import jax
import jax.numpy as jnp
import numpy as np
from jax import lax
from jax.experimental import pallas as pl
from jax.experimental.pallas import tpu as pltpu
from jax.sharding import PartitionSpec as P

ITERS = 4
MESH = pl.DeviceIdType.MESH

first_tau = np.float32(0.35)
step_product = np.float32(0.124)
adapt_rate = 0.5
adapt_decay = 0.9
epsilon = np.float32(1e-06)

SUB = 8
LANE = 128
UNROLL = 3


def kernel(
    n_row, n_col, cells,
    noisy_hbm, fid_hbm,
    u_out, dual_out, tau_out,
    N, F, U, H, UB, PX, PY, GX, GY, DV, QT, CB, rb,
    load_sem, halo_send, halo_recv, red_send, red_recv,
):
    rows, cols = noisy_hbm.shape
    strips = rows // SUB + 2
    tiles = cols // LANE
    my_row, my_col = lax.axis_index("row"), lax.axis_index("col")
    f32 = jnp.float32

    def distance(ab):
        a, b = ab
        return sum(min(v % 4, 4 - v % 4) for v in (a // 2, b // 4, b % 4))

    def row_at(d):
        return lax.rem(my_row + d + n_row, n_row)

    def col_at(d):
        return lax.rem(my_col + d + n_col, n_col)

    sub = lax.broadcasted_iota(jnp.int32, (SUB, LANE), 0)
    lane = lax.broadcasted_iota(jnp.int32, (SUB, LANE), 1)
    sub_first, sub_last = sub == 0, sub == SUB - 1
    lane_first, lane_last = lane == 0, lane == LANE - 1

    def at(s, c):
        start = s * SUB if isinstance(s, int) else pl.multiple_of(s * SUB, SUB)
        return pl.ds(start, SUB), slice(c * LANE, (c + 1) * LANE)

    at_left, at_right = my_col == 0, my_col == n_col - 1
    last_col = jnp.logical_and(at_right, lane_last)
    outside = jnp.logical_and(at_left, lane >= LANE // 2)
    in_first_row = jnp.logical_and(my_row == 0, sub_first)

    def gradient_strip(field, s, which):
        cell = my_row * rows + (s - 1) * SUB + sub
        inside = jnp.logical_and(cell >= 0, cell < n_row * rows - 1)
        after = min(s + 1, strips - 1) if isinstance(s, int) else jnp.minimum(s + 1, strips - 1)
        here = {c: field[at(s, c)] for c in {c for w in which for c in (w, (w + 1) % (tiles + 1))}}
        turned = {c: pltpu.roll(h, LANE - 1, axis=1) for c, h in here.items()}
        for c in which:
            below = jnp.where(
                sub_last,
                pltpu.roll(field[at(after, c)], SUB - 1, axis=0),
                pltpu.roll(here[c], SUB - 1, axis=0),
            )
            right = jnp.where(lane_last, turned[(c + 1) % (tiles + 1)], turned[c])
            gx = jnp.where(inside, below - here[c], 0.0)
            gy = right - here[c]
            if c == tiles - 1:
                gy = jnp.where(last_col, 0.0, gy)
            if c == tiles:
                gy = jnp.where(outside, 0.0, gy)
            GX[at(s, c)] = gx
            GY[at(s, c)] = gy

    everywhere = tuple(range(tiles + 1))

    def between(s, carry):
        gradient_strip(UB, s, everywhere)
        for c in everywhere:
            H[at(s, c)] = F[at(s, c)] * (U[at(s, c)] - N[at(s, c)])
        return carry

    CB[...] = jnp.zeros_like(CB)

    loads = [
        pltpu.make_async_copy(src, dst.at[SUB : SUB + rows, 0:cols], load_sem.at[i])
        for i, (src, dst) in enumerate(((noisy_hbm, N), (fid_hbm, F)))
    ]
    for load in loads:
        load.start()
    barrier = pltpu.get_barrier_semaphore()
    offsets = [(a, b) for a in range(n_row) for b in range(n_col) if a or b]
    offsets.sort(key=lambda ab: -distance(ab))
    partners = [(row_at(a), col_at(b)) for a, b in offsets]
    for partner in partners:
        pl.semaphore_signal(barrier, inc=1, device_id=partner, device_id_type=MESH)
    for load in loads:
        load.wait()

    def pack(b):
        at = pl.ds(SUB + b * LANE, LANE)
        lanes = lax.broadcasted_iota(jnp.int32, (LANE, LANE), 1)
        n0, n7 = N[at, 0:LANE], N[at, cols - LANE : cols]
        f0 = pltpu.roll(F[at, 0:LANE], 8, axis=1)
        f7 = pltpu.roll(F[at, cols - LANE : cols], LANE - 8, axis=1)
        low = jnp.where(lanes < 8, n0, f0)
        high = jnp.where(lanes >= LANE - 8, n7, f7)
        return jnp.where(lanes < LANE // 2, low, high).T

    for b in range(rows // LANE):
        QT[:, b * LANE : (b + 1) * LANE] = pack(b)

    pl.semaphore_wait(barrier, len(partners))

    low, high = slice(0, 16), slice(LANE - 16, LANE)
    mid = slice(LANE, LANE + rows)
    top, bottom = slice(0, LANE), slice(LANE + rows, 2 * LANE + rows)
    first, last = slice(0, LANE), slice(rows - LANE, rows)
    below_rows = slice(rows + SUB, rows + 2 * SUB)
    moves = []
    for src, dst in ((noisy_hbm, N), (fid_hbm, F)):
        moves.append((src.at[0:SUB, :], dst.at[below_rows, 0:cols], -1, 0))
        moves.append((src.at[rows - SUB : rows, :], dst.at[0:SUB, 0:cols], 1, 0))
    moves.append((QT.at[low, :], CB.at[low, mid], 0, -1))
    moves.append((QT.at[high, :], CB.at[high, mid], 0, 1))
    for side, step in ((low, -1), (high, 1)):
        moves.append((QT.at[side, last], CB.at[side, top], 1, step))
        moves.append((QT.at[side, first], CB.at[side, bottom], -1, step))
    halos = [
        pltpu.make_async_remote_copy(
            src_ref=src, dst_ref=dst, send_sem=halo_send.at[i], recv_sem=halo_recv.at[i],
            device_id=(row_at(a), col_at(b)), device_id_type=MESH,
        )
        for i, (src, dst, a, b) in enumerate(moves)
    ]
    for halo in halos:
        halo.start()

    def interior(s, carry):
        gradient_strip(N, s, everywhere[: tiles - 1])
        return carry

    lax.fori_loop(1, strips - 2, interior, 0)

    for halo in halos:
        halo.wait_recv()

    def unpack(block, start, count, to):
        turned = block.T[start : start + count, :]
        lanes = lax.broadcasted_iota(jnp.int32, turned.shape, 1)
        edge = jnp.logical_or(lanes < 8, lanes >= LANE - 8)
        fid = jnp.where(
            lanes < LANE // 2, pltpu.roll(turned, LANE - 8, axis=1), pltpu.roll(turned, 8, axis=1)
        )
        N[to : to + count, cols : cols + LANE] = jnp.where(edge, turned, 0.0)
        F[to : to + count, cols : cols + LANE] = jnp.where(edge, fid, 1.0)

    unpack(CB[:, top], LANE - SUB, SUB, 0)
    for b in range(rows // LANE):
        unpack(CB[:, (b + 1) * LANE : (b + 2) * LANE], 0, LANE, SUB + b * LANE)
    unpack(CB[:, bottom], 0, SUB, SUB + rows)

    def border(s, carry):
        gradient_strip(N, s, everywhere[tiles - 1 :])
        return carry

    lax.fori_loop(1, strips - 2, border, 0)
    for s in (0, strips - 2, strips - 1):
        gradient_strip(N, s, everywhere)

    def strip(k, s, carry, counted, tau, sigma, itau, isigma):
        prev_x, prev_w, acc_p, acc_d, acc_l = carry
        prev_x, prev_w = list(prev_x), list(prev_w)
        final = k == ITERS - 1
        first_strip = isinstance(s, int) and s == 1

        def dual_step(c):
            qx, qy = sigma * GX[at(s, c)], sigma * GY[at(s, c)]
            if k:
                px, py = PX[at(s, c)], PY[at(s, c)]
                qx, qy = px + qx, py + qy
            scale = lax.rsqrt(jnp.maximum(qx * qx + qy * qy, 1.0))
            nx, ny = qx * scale, qy * scale
            tx, ty = (px - nx, py - ny) if k else (-nx, -ny)
            return nx, ny, tx, ty, pltpu.roll(nx, 1, axis=0), pltpu.roll(ny, 1, axis=1)

        def primal_step(c, dual, left):
            nx, ny, tx, ty, rx, ry = dual
            div = (nx - jnp.where(sub_first, prev_x[c], rx)) + (ny - jnp.where(lane_first, left, ry))
            prev_x[c] = rx
            if k:
                old = U[at(s, c)]
                du = (H[at(s, c)] - div) / (itau + F[at(s, c)])
            else:
                old = N[at(s, c)]
                du = div / (-itau - F[at(s, c)])
            new = old - du
            scaled = sigma * du
            wx, wy = tx + scaled, ty + scaled
            before = DV[at(s, c)] if k and counted and c < tiles else None
            if not final:
                PX[at(s, c)] = nx
                PY[at(s, c)] = ny
                U[at(s, c)] = new
                UB[at(s, c)] = new - du
                if c < tiles:
                    DV[at(s, c)] = div
            elif counted and c < tiles:
                own = at(s - 1, c)
                u_out[own] = new
                dual_out[(0, *own)] = nx
                dual_out[(1, *own)] = ny
            rwx, rwy = pltpu.roll(wx, 1, axis=0), pltpu.roll(wy, 1, axis=1)
            upper = prev_w[c]
            prev_w[c] = rwx
            return div, du, scaled, before, upper, rwx, rwy

        def residual(got, left):
            div, du, scaled, before, upper, rwx, rwy = got
            primal = du * itau - div
            if before is not None:
                primal = primal + before
            return (
                jnp.abs(primal),
                jnp.abs(jnp.where(sub_first, upper, rwx) - scaled),
                jnp.abs(jnp.where(lane_first, left, rwy) - scaled),
            )

        before_last = dual_step(tiles - 1)
        halo = dual_step(tiles)
        halo_got = primal_step(tiles, halo, before_last[5])
        left, left_w = halo[5], halo_got[6]
        for c in range(tiles):
            dual = before_last if c == tiles - 1 else dual_step(c)
            got = primal_step(c, dual, left)
            if counted:
                primal, along, across = residual(got, left_w)
                if first_strip:
                    along = jnp.where(in_first_row, 0.0, along)
                acc_p = acc_p + primal
                if c == 0:
                    acc_l = acc_l + across
                    acc_d = acc_d + along
                else:
                    acc_d = acc_d + (along + across)
            left, left_w = dual[5], got[6]
        return tuple(prev_x), tuple(prev_w), acc_p, acc_d, acc_l

    me = my_row * n_col + my_col
    others = len(offsets)

    def reduce_start(k, primal, dual):
        rb[k, me, 0:1, :] = jnp.sum(primal, axis=0, keepdims=True)
        rb[k, me, 1:2, :] = jnp.sum(dual, axis=0, keepdims=True)
        for partner in partners:
            pltpu.make_async_remote_copy(
                src_ref=rb.at[k, me], dst_ref=rb.at[k, me],
                send_sem=red_send.at[k], recv_sem=red_recv.at[k],
                device_id=partner, device_id_type=MESH,
            ).start()

    def reduce_end(k):
        got = rb.at[k, 0:others]
        pltpu.make_async_copy(got, got, red_recv.at[k]).wait()
        parts = [rb[k, i] for i in range(others + 1)]
        while len(parts) > 1:
            parts = [a + b for a, b in zip(parts[::2], parts[1::2])]
        total = jnp.sum(parts[0], axis=1, keepdims=True)
        return total[0:1], total[1:2]

    zero = jnp.zeros((SUB, LANE), f32)
    tau_one = jnp.full((1, 1), first_tau, f32)
    sigma_one = jnp.full((1, 1), step_product / first_tau, f32)
    for k in range(ITERS):
        def full(x):
            return jnp.broadcast_to(x, (SUB, LANE))

        steps = (full(tau_one), full(sigma_one), full(1.0 / tau_one), full(1.0 / sigma_one))
        none = (zero,) * (tiles + 1)
        carry = strip(k, 0, (none, none, zero, zero, zero), False, *steps)
        carry = strip(k, 1, carry, True, *steps)

        def body(i, carry, k=k, steps=steps):
            for j in range(UNROLL):
                carry = strip(k, 2 + i * UNROLL + j, carry, True, *steps)
            return carry

        whole = (strips - 3) // UNROLL
        carry = lax.fori_loop(0, whole, body, carry)
        for s in range(2 + whole * UNROLL, strips - 1):
            carry = strip(k, s, carry, True, *steps)
        if k < ITERS - 1:
            carry = strip(k, strips - 1, carry, False, *steps)
        _, _, primal, dual, at_first = carry
        dual = dual + jnp.where(jnp.logical_and(at_left, lane_first), 0.0, at_first)
        reduce_start(k, primal, dual * steps[3])
        if k < ITERS - 1:
            lax.fori_loop(0, strips, between, 0)
        primal, dual = reduce_end(k)
        ratio = jnp.log((primal / cells + epsilon) / (dual / cells + epsilon))
        rate = np.float32(adapt_rate * adapt_decay**k)
        tau_one = tau_one * jnp.exp(rate * ratio / (1.0 + jnp.abs(ratio)))
        sigma_one = step_product / tau_one
    tau_out[...] = jnp.broadcast_to(tau_one, tau_out.shape)

    for halo in halos:
        halo.wait_send()
    for k in range(ITERS):
        sent = rb.at[k, 0:others]
        pltpu.make_async_copy(sent, sent, red_send.at[k]).wait()


def solution(mesh):
    n_row, n_col = mesh.shape["row"], mesh.shape["col"]

    def on_device(noisy, fidelity):
        rows, cols = noisy.shape
        f32 = jnp.float32
        padded = pltpu.VMEM((rows + 2 * SUB, cols + LANE), f32)
        cells = np.float32(rows * cols * n_row * n_col)
        vmem = pl.BlockSpec(memory_space=pltpu.VMEM)
        current, dual, tau = pl.pallas_call(
            functools.partial(kernel, n_row, n_col, cells),
            out_shape=(
                jax.ShapeDtypeStruct((rows, cols), f32),
                jax.ShapeDtypeStruct((2, rows, cols), f32),
                jax.ShapeDtypeStruct((1, LANE), f32),
            ),
            in_specs=[pl.BlockSpec(memory_space=pl.ANY)] * 2,
            out_specs=(vmem, vmem, vmem),
            scratch_shapes=[padded] * 10
            + [
                pltpu.VMEM((LANE, rows), f32),
                pltpu.VMEM((LANE, rows + 2 * LANE), f32),
                pltpu.VMEM((ITERS, n_row * n_col, 2, LANE), f32),
                pltpu.SemaphoreType.DMA((2,)),
                pltpu.SemaphoreType.DMA((10,)),
                pltpu.SemaphoreType.DMA((10,)),
                pltpu.SemaphoreType.DMA((ITERS,)),
                pltpu.SemaphoreType.DMA((ITERS,)),
            ],
            compiler_params=pltpu.CompilerParams(
                collective_id=0, has_side_effects=True, vmem_limit_bytes=40 * 1024 * 1024
            ),
        )(*(pltpu.with_memory_space_constraint(x, pltpu.HBM) for x in (noisy, fidelity)))
        return current, dual, tau[0, 0]

    return jax.shard_map(
        on_device,
        mesh=mesh,
        in_specs=(P("row", "col"), P("row", "col")),
        out_specs=(P("row", "col"), P(None, "row", "col"), P()),
        check_vma=False,
    )
```

time: 65.9 us -> 57.5 us (0.87)
  Pallas kernels: 59.1 us -> 53.3 us
  local copies, waits for them, and re-layouts: 4.73 us -> 2.29 us
    pallas_call x1, Pallas kernels: 59.1 us -> 53.3 us  [on_device(): pl.pallas_call(functools.partial(kernel, n_row, n_col, cells), out_shape=...]
    unnamed x6 -> x2, local copies, waits for them, and re-layouts: 4.73 us -> 2.29 us
where the time goes in v2:
time: 57.5 us; the launch traced here: 57.3 us
  Pallas kernels  53.3 us (93%)
  local copies, waits for them, and re-layouts  2.29 us (4%)
  between operations  1.8 us (3%)
    pallas_call x1, Pallas kernels, on_device(): pl.pallas_call(functools.partial(kernel, n_row, n_col, cells), out_shape=...  53.3 us
    unnamed x2, local copies, waits for them, and re-layouts  2.29 us

profile of v2, /device:TPU:1, one launch (start us, length us, event | category | flops | bytes accessed | tf_op | source)
XLA Modules:
  0.0 57.3 jit_solution(14477967501252020282)
XLA Ops:
  0.6 53.3 %shard_map.49 = (f32[256,1024]{1,0:T(8,128)S(1)}, f32[2,256,1024]{2,1,0:T(8,128)S(1)}, f32[1,128]{1,0:T(1,128)S(1)}) custom-call(f32[256,1024]{1,0:T(8,128)} %noisy_hbm.1, f32[256,1024]{1,0:T(8,128)} %fid_hbm.1), custom_call_target="tpu_custom_call" | custom-call | tf_op jit(solution)/shard_map/pallas_call | solution.py:330
  53.9 1.0 %copy.8 = f32[256,1024]{1,0:T(8,128)} copy(f32[256,1024]{1,0:T(8,128)S(1)} %get-tuple-element.12) | data formatting | bytes 2097152
  54.9 1.3 %copy.9 = f32[2,256,1024]{2,1,0:T(8,128)} copy(f32[2,256,1024]{2,1,0:T(8,128)S(1)} %get-tuple-element.13) | data formatting | bytes 4194304

commit v3 on v2

--- a/solution.py
+++ b/solution.py
@@ -18,7 +18,7 @@
 
 SUB = 8
 LANE = 128
-UNROLL = 3
+UNROLL = 5
 
 
 def kernel(
@@ -26,7 +26,7 @@
     noisy_hbm, fid_hbm,
     u_out, dual_out, tau_out,
     N, F, U, H, UB, PX, PY, GX, GY, DV, QT, CB, rb,
-    load_sem, halo_send, halo_recv, red_send, red_recv,
+    load_sem, halo_send, halo_recv, red_send, red_recv, known,
 ):
     rows, cols = noisy_hbm.shape
     strips = rows // SUB + 2
@@ -90,20 +90,33 @@
 
     CB[...] = jnp.zeros_like(CB)
 
-    loads = [
-        pltpu.make_async_copy(src, dst.at[SUB : SUB + rows, 0:cols], load_sem.at[i])
-        for i, (src, dst) in enumerate(((noisy_hbm, N), (fid_hbm, F)))
+    own = slice(SUB, SUB + rows)
+    edges, inner = [], []
+    for i, (src, dst) in enumerate(((noisy_hbm, N), (fid_hbm, F))):
+        for j, (part, group) in enumerate((
+            (slice(0, LANE), edges), (slice(cols - LANE, cols), edges), (slice(LANE, cols - LANE), inner),
+        )):
+            group.append(pltpu.make_async_copy(src.at[:, part], dst.at[own, part], load_sem.at[i, j]))
+    for load in edges + inner:
+        load.start()
+
+    around = [(a, b) for a in (-1, 0, 1) for b in (-1, 0, 1) if a or b]
+    barrier = pltpu.get_barrier_semaphore()
+    for a, b in around:
+        pl.semaphore_signal(barrier, inc=1, device_id=(row_at(a), col_at(b)), device_id_type=MESH)
+
+    rounds = [
+        around,
+        [(2 * a, 2 * b) for a, b in around],
+        [(0, -4), (0, 4)],
     ]
-    for load in loads:
-        load.start()
-    barrier = pltpu.get_barrier_semaphore()
-    offsets = [(a, b) for a in range(n_row) for b in range(n_col) if a or b]
-    offsets.sort(key=lambda ab: -distance(ab))
-    partners = [(row_at(a), col_at(b)) for a, b in offsets]
-    for partner in partners:
-        pl.semaphore_signal(barrier, inc=1, device_id=partner, device_id_type=MESH)
-    for load in loads:
-        load.wait()
+
+    def tell(i):
+        for a, b in rounds[i]:
+            pl.semaphore_signal(known.at[i], inc=1, device_id=(row_at(a), col_at(b)), device_id_type=MESH)
+
+    def learn(i):
+        pl.semaphore_wait(known.at[i], len(rounds[i]))
 
     def pack(b):
         at = pl.ds(SUB + b * LANE, LANE)
@@ -114,11 +127,6 @@
         low = jnp.where(lanes < 8, n0, f0)
         high = jnp.where(lanes >= LANE - 8, n7, f7)
         return jnp.where(lanes < LANE // 2, low, high).T
-
-    for b in range(rows // LANE):
-        QT[:, b * LANE : (b + 1) * LANE] = pack(b)
-
-    pl.semaphore_wait(barrier, len(partners))
 
     low, high = slice(0, 16), slice(LANE - 16, LANE)
     mid = slice(LANE, LANE + rows)
@@ -141,8 +149,18 @@
         )
         for i, (src, dst, a, b) in enumerate(moves)
     ]
-    for halo in halos:
+    pl.semaphore_wait(barrier, len(around))
+    for halo in halos[:4]:
         halo.start()
+    for load in edges:
+        load.wait()
+    for b in range(rows // LANE):
+        QT[:, b * LANE : (b + 1) * LANE] = pack(b)
+    for halo in halos[4:]:
+        halo.start()
+    tell(0)
+    for load in inner:
+        load.wait()
 
     def interior(s, carry):
         gradient_strip(N, s, everywhere[: tiles - 1])
@@ -152,6 +170,8 @@
 
     for halo in halos:
         halo.wait_recv()
+    learn(0)
+    tell(1)
 
     def unpack(block, start, count, to):
         turned = block.T[start : start + count, :]
@@ -254,6 +274,9 @@
             left, left_w = dual[5], got[6]
         return tuple(prev_x), tuple(prev_w), acc_p, acc_d, acc_l
 
+    offsets = [(a, b) for a in range(n_row) for b in range(n_col) if a or b]
+    offsets.sort(key=lambda ab: -distance(ab))
+    partners = [(row_at(a), col_at(b)) for a, b in offsets]
     me = my_row * n_col + my_col
     others = len(offsets)
 
@@ -294,7 +317,14 @@
             return carry
 
         whole = (strips - 3) // UNROLL
-        carry = lax.fori_loop(0, whole, body, carry)
+        if k == 0:
+            carry = lax.fori_loop(0, whole // 2, body, carry)
+            learn(1)
+            tell(2)
+            carry = lax.fori_loop(whole // 2, whole, body, carry)
+            learn(2)
+        else:
+            carry = lax.fori_loop(0, whole, body, carry)
         for s in range(2 + whole * UNROLL, strips - 1):
             carry = strip(k, s, carry, True, *steps)
         if k < ITERS - 1:
@@ -341,11 +371,12 @@
                 pltpu.VMEM((LANE, rows), f32),
                 pltpu.VMEM((LANE, rows + 2 * LANE), f32),
                 pltpu.VMEM((ITERS, n_row * n_col, 2, LANE), f32),
-                pltpu.SemaphoreType.DMA((2,)),
+                pltpu.SemaphoreType.DMA((2, 3)),
                 pltpu.SemaphoreType.DMA((10,)),
                 pltpu.SemaphoreType.DMA((10,)),
                 pltpu.SemaphoreType.DMA((ITERS,)),
                 pltpu.SemaphoreType.DMA((ITERS,)),
+                pltpu.SemaphoreType.REGULAR((3,)),
             ],
             compiler_params=pltpu.CompilerParams(
                 collective_id=0, has_side_effects=True, vmem_limit_bytes=40 * 1024 * 1024

time: 57.5 us -> 55.9 us (0.972)
  Pallas kernels: 53.3 us -> 51.6 us
    pallas_call x1, Pallas kernels: 53.3 us -> 51.6 us  [on_device(): pl.pallas_call(functools.partial(kernel, n_row, n_col, cells), out_shape=...]
where the time goes in v3:
time: 55.9 us; the launch traced here: 55.7 us
  Pallas kernels  51.6 us (92%)
  local copies, waits for them, and re-layouts  2.29 us (4%)
  between operations  1.8 us (3%)
    pallas_call x1, Pallas kernels, on_device(): pl.pallas_call(functools.partial(kernel, n_row, n_col, cells), out_shape=...  51.6 us
    unnamed x2, local copies, waits for them, and re-layouts  2.29 us

profile of v3, /device:TPU:1, one launch (start us, length us, event | category | flops | bytes accessed | tf_op | source)
XLA Modules:
  0.0 55.7 jit_solution(6438434646244224137)
XLA Ops:
  0.6 51.6 %shard_map.49 = (f32[256,1024]{1,0:T(8,128)S(1)}, f32[2,256,1024]{2,1,0:T(8,128)S(1)}, f32[1,128]{1,0:T(1,128)S(1)}) custom-call(f32[256,1024]{1,0:T(8,128)} %noisy_hbm.1, f32[256,1024]{1,0:T(8,128)} %fid_hbm.1), custom_call_target="tpu_custom_call" | custom-call | tf_op jit(solution)/shard_map/pallas_call | solution.py:360
  52.3 1.0 %copy.8 = f32[256,1024]{1,0:T(8,128)} copy(f32[256,1024]{1,0:T(8,128)S(1)} %get-tuple-element.12) | data formatting | bytes 2097152
  53.3 1.3 %copy.9 = f32[2,256,1024]{2,1,0:T(8,128)} copy(f32[2,256,1024]{2,1,0:T(8,128)S(1)} %get-tuple-element.13) | data formatting | bytes 4194304

commit v4 on v3

--- a/solution.py
+++ b/solution.py
@@ -8,6 +8,7 @@
 from jax.sharding import PartitionSpec as P
 
 ITERS = 4
+SIDE = 4
 MESH = pl.DeviceIdType.MESH
 
 first_tau = np.float32(0.35)
@@ -18,14 +19,14 @@
 
 SUB = 8
 LANE = 128
-UNROLL = 5
+UNROLL = 6
 
 
 def kernel(
     n_row, n_col, cells,
     noisy_hbm, fid_hbm,
     u_out, dual_out, tau_out,
-    N, F, U, H, UB, PX, PY, GX, GY, DV, QT, CB, rb,
+    N, F, U, H, UB, DU, PX, PY, GX, GY, DV, QT, CB, rb,
     load_sem, halo_send, halo_recv, red_send, red_recv, known,
 ):
     rows, cols = noisy_hbm.shape
@@ -82,11 +83,29 @@
 
     everywhere = tuple(range(tiles + 1))
 
-    def between(s, carry):
-        gradient_strip(UB, s, everywhere)
-        for c in everywhere:
-            H[at(s, c)] = F[at(s, c)] * (U[at(s, c)] - N[at(s, c)])
-        return carry
+    def over_strips(first, end, group, work):
+        def body(i, carry):
+            for j in range(group):
+                work(first + i * group + j)
+            return carry
+
+        trips = (end - first) // group
+        if trips:
+            lax.fori_loop(0, trips, body, 0)
+        for s in range(first + trips * group, end):
+            work(s)
+
+    def between(k):
+        def advance(s):
+            for c in everywhere:
+                du, noisy = DU[at(s, c)], N[at(s, c)]
+                new = (U[at(s, c)] if k else noisy) - du
+                U[at(s, c)] = new
+                UB[at(s, c)] = new - du
+                H[at(s, c)] = F[at(s, c)] * (new - noisy)
+
+        over_strips(0, strips, 2, advance)
+        over_strips(0, strips, 4, lambda s: gradient_strip(UB, s, everywhere))
 
     CB[...] = jnp.zeros_like(CB)
 
@@ -100,23 +119,23 @@
     for load in edges + inner:
         load.start()
 
-    around = [(a, b) for a in (-1, 0, 1) for b in (-1, 0, 1) if a or b]
+    def chip_at(y, core, z, x):
+        row = lax.rem(my_row // 2 + y + SIDE, SIDE) * 2 + lax.rem(my_row + core, 2)
+        col = lax.rem(my_col // SIDE + z + SIDE, SIDE) * SIDE + lax.rem(my_col + x + SIDE, SIDE)
+        return row, col
+
+    near = (-1, 0, 1)
+    around = [(y, c, z, x) for y in near for c in (0, 1) for z in near for x in near if y or c or z or x]
+    around.sort(key=lambda at: -sum(abs(v) for v in at))
     barrier = pltpu.get_barrier_semaphore()
-    for a, b in around:
-        pl.semaphore_signal(barrier, inc=1, device_id=(row_at(a), col_at(b)), device_id_type=MESH)
-
-    rounds = [
-        around,
-        [(2 * a, 2 * b) for a, b in around],
-        [(0, -4), (0, 4)],
-    ]
-
-    def tell(i):
-        for a, b in rounds[i]:
-            pl.semaphore_signal(known.at[i], inc=1, device_id=(row_at(a), col_at(b)), device_id_type=MESH)
-
-    def learn(i):
-        pl.semaphore_wait(known.at[i], len(rounds[i]))
+    for where in around:
+        pl.semaphore_signal(barrier, inc=1, device_id=chip_at(*where), device_id_type=MESH)
+
+    corners = [(y, 0, z, x) for y in (-1, 1) for z in (-1, 1) for x in (-1, 1)]
+
+    def tell():
+        for where in corners:
+            pl.semaphore_signal(known, inc=1, device_id=chip_at(*where), device_id_type=MESH)
 
     def pack(b):
         at = pl.ds(SUB + b * LANE, LANE)
@@ -150,6 +169,7 @@
         for i, (src, dst, a, b) in enumerate(moves)
     ]
     pl.semaphore_wait(barrier, len(around))
+    tell()
     for halo in halos[:4]:
         halo.start()
     for load in edges:
@@ -158,20 +178,13 @@
         QT[:, b * LANE : (b + 1) * LANE] = pack(b)
     for halo in halos[4:]:
         halo.start()
-    tell(0)
     for load in inner:
         load.wait()
 
-    def interior(s, carry):
-        gradient_strip(N, s, everywhere[: tiles - 1])
-        return carry
-
-    lax.fori_loop(1, strips - 2, interior, 0)
+    over_strips(1, strips - 2, 4, lambda s: gradient_strip(N, s, everywhere[: tiles - 1]))
 
     for halo in halos:
         halo.wait_recv()
-    learn(0)
-    tell(1)
 
     def unpack(block, start, count, to):
         turned = block.T[start : start + count, :]
@@ -188,11 +201,7 @@
         unpack(CB[:, (b + 1) * LANE : (b + 2) * LANE], 0, LANE, SUB + b * LANE)
     unpack(CB[:, bottom], 0, SUB, SUB + rows)
 
-    def border(s, carry):
-        gradient_strip(N, s, everywhere[tiles - 1 :])
-        return carry
-
-    lax.fori_loop(1, strips - 2, border, 0)
+    over_strips(1, strips - 2, 16, lambda s: gradient_strip(N, s, everywhere[tiles - 1 :]))
     for s in (0, strips - 2, strips - 1):
         gradient_strip(N, s, everywhere)
 
@@ -217,25 +226,20 @@
             div = (nx - jnp.where(sub_first, prev_x[c], rx)) + (ny - jnp.where(lane_first, left, ry))
             prev_x[c] = rx
             if k:
-                old = U[at(s, c)]
                 du = (H[at(s, c)] - div) / (itau + F[at(s, c)])
             else:
-                old = N[at(s, c)]
                 du = div / (-itau - F[at(s, c)])
-            new = old - du
+            DU[at(s, c)] = du
             scaled = sigma * du
             wx, wy = tx + scaled, ty + scaled
             before = DV[at(s, c)] if k and counted and c < tiles else None
             if not final:
                 PX[at(s, c)] = nx
                 PY[at(s, c)] = ny
-                U[at(s, c)] = new
-                UB[at(s, c)] = new - du
                 if c < tiles:
                     DV[at(s, c)] = div
             elif counted and c < tiles:
                 own = at(s - 1, c)
-                u_out[own] = new
                 dual_out[(0, *own)] = nx
                 dual_out[(1, *own)] = ny
             rwx, rwy = pltpu.roll(wx, 1, axis=0), pltpu.roll(wy, 1, axis=1)
@@ -299,6 +303,10 @@
         total = jnp.sum(parts[0], axis=1, keepdims=True)
         return total[0:1], total[1:2]
 
+    def finish(s):
+        for c in range(tiles):
+            u_out[at(s - 1, c)] = U[at(s, c)] - DU[at(s, c)]
+
     zero = jnp.zeros((SUB, LANE), f32)
     tau_one = jnp.full((1, 1), first_tau, f32)
     sigma_one = jnp.full((1, 1), step_product / first_tau, f32)
@@ -317,23 +325,19 @@
             return carry
 
         whole = (strips - 3) // UNROLL
-        if k == 0:
-            carry = lax.fori_loop(0, whole // 2, body, carry)
-            learn(1)
-            tell(2)
-            carry = lax.fori_loop(whole // 2, whole, body, carry)
-            learn(2)
-        else:
-            carry = lax.fori_loop(0, whole, body, carry)
+        carry = lax.fori_loop(0, whole, body, carry)
         for s in range(2 + whole * UNROLL, strips - 1):
             carry = strip(k, s, carry, True, *steps)
-        if k < ITERS - 1:
-            carry = strip(k, strips - 1, carry, False, *steps)
         _, _, primal, dual, at_first = carry
         dual = dual + jnp.where(jnp.logical_and(at_left, lane_first), 0.0, at_first)
+        if k == 0:
+            pl.semaphore_wait(known, len(corners))
         reduce_start(k, primal, dual * steps[3])
         if k < ITERS - 1:
-            lax.fori_loop(0, strips, between, 0)
+            strip(k, strips - 1, carry, False, *steps)
+            between(k)
+        else:
+            over_strips(1, strips - 1, 4, finish)
         primal, dual = reduce_end(k)
         ratio = jnp.log((primal / cells + epsilon) / (dual / cells + epsilon))
         rate = np.float32(adapt_rate * adapt_decay**k)
@@ -366,7 +370,7 @@
             ),
             in_specs=[pl.BlockSpec(memory_space=pl.ANY)] * 2,
             out_specs=(vmem, vmem, vmem),
-            scratch_shapes=[padded] * 10
+            scratch_shapes=[padded] * 11
             + [
                 pltpu.VMEM((LANE, rows), f32),
                 pltpu.VMEM((LANE, rows + 2 * LANE), f32),
@@ -376,7 +380,7 @@
                 pltpu.SemaphoreType.DMA((10,)),
                 pltpu.SemaphoreType.DMA((ITERS,)),
                 pltpu.SemaphoreType.DMA((ITERS,)),
-                pltpu.SemaphoreType.REGULAR((3,)),
+                pltpu.SemaphoreType.REGULAR,
             ],
             compiler_params=pltpu.CompilerParams(
                 collective_id=0, has_side_effects=True, vmem_limit_bytes=40 * 1024 * 1024

time: 55.9 us -> 52.3 us (0.936)
  Pallas kernels: 51.6 us -> 48.1 us
    pallas_call x1, Pallas kernels: 51.6 us -> 48.1 us  [on_device(): pl.pallas_call(functools.partial(kernel, n_row, n_col, cells), out_shape=...]
where the time goes in v4:
time: 52.3 us; the launch traced here: 52.2 us
  Pallas kernels  48.1 us (92%)
  local copies, waits for them, and re-layouts  2.29 us (4%)
  between operations  1.8 us (3%)
    pallas_call x1, Pallas kernels, on_device(): pl.pallas_call(functools.partial(kernel, n_row, n_col, cells), out_shape=...  48.1 us
    unnamed x2, local copies, waits for them, and re-layouts  2.29 us

profile of v4, /device:TPU:1, one launch (start us, length us, event | category | flops | bytes accessed | tf_op | source)
XLA Modules:
  0.0 52.2 jit_solution(11532793788547771248)
XLA Ops:
  0.6 48.1 %shard_map.49 = (f32[256,1024]{1,0:T(8,128)S(1)}, f32[2,256,1024]{2,1,0:T(8,128)S(1)}, f32[1,128]{1,0:T(1,128)S(1)}) custom-call(f32[256,1024]{1,0:T(8,128)} %noisy_hbm.1, f32[256,1024]{1,0:T(8,128)} %fid_hbm.1), custom_call_target="tpu_custom_call" | custom-call | tf_op jit(solution)/shard_map/pallas_call | solution.py:364
  48.7 1.0 %copy.8 = f32[256,1024]{1,0:T(8,128)} copy(f32[256,1024]{1,0:T(8,128)S(1)} %get-tuple-element.12) | data formatting | bytes 2097152
  49.7 1.3 %copy.9 = f32[2,256,1024]{2,1,0:T(8,128)} copy(f32[2,256,1024]{2,1,0:T(8,128)S(1)} %get-tuple-element.13) | data formatting | bytes 4194304

commit v5 on v4

--- a/solution.py
+++ b/solution.py
@@ -107,8 +107,6 @@
         over_strips(0, strips, 2, advance)
         over_strips(0, strips, 4, lambda s: gradient_strip(UB, s, everywhere))
 
-    CB[...] = jnp.zeros_like(CB)
-
     own = slice(SUB, SUB + rows)
     edges, inner = [], []
     for i, (src, dst) in enumerate(((noisy_hbm, N), (fid_hbm, F))):
@@ -118,6 +116,8 @@
             group.append(pltpu.make_async_copy(src.at[:, part], dst.at[own, part], load_sem.at[i, j]))
     for load in edges + inner:
         load.start()
+
+    CB[...] = jnp.zeros_like(CB)
 
     def chip_at(y, core, z, x):
         row = lax.rem(my_row // 2 + y + SIDE, SIDE) * 2 + lax.rem(my_row + core, 2)
@@ -285,8 +285,9 @@
     others = len(offsets)
 
     def reduce_start(k, primal, dual):
-        rb[k, me, 0:1, :] = jnp.sum(primal, axis=0, keepdims=True)
-        rb[k, me, 1:2, :] = jnp.sum(dual, axis=0, keepdims=True)
+        half = LANE // 2
+        both = jnp.where(lane < half, primal + pltpu.roll(primal, half, axis=1), dual + pltpu.roll(dual, half, axis=1))
+        rb[k, me] = jnp.sum(both, axis=0, keepdims=True)
         for partner in partners:
             pltpu.make_async_remote_copy(
                 src_ref=rb.at[k, me], dst_ref=rb.at[k, me],
@@ -300,8 +301,10 @@
         parts = [rb[k, i] for i in range(others + 1)]
         while len(parts) > 1:
             parts = [a + b for a, b in zip(parts[::2], parts[1::2])]
-        total = jnp.sum(parts[0], axis=1, keepdims=True)
-        return total[0:1], total[1:2]
+        lower = lax.broadcasted_iota(jnp.int32, (1, LANE), 1) < LANE // 2
+        primal = jnp.sum(jnp.where(lower, parts[0], 0.0), axis=1, keepdims=True)
+        dual = jnp.sum(jnp.where(lower, 0.0, parts[0]), axis=1, keepdims=True)
+        return primal, dual
 
     def finish(s):
         for c in range(tiles):
@@ -352,6 +355,27 @@
         pltpu.make_async_copy(sent, sent, red_send.at[k]).wait()
 
 
+def write_kernel(u_ref, dual_ref, u_hbm, dual_hbm, sem):
+    moves = [(u_ref, u_hbm), (dual_ref.at[0], dual_hbm.at[0]), (dual_ref.at[1], dual_hbm.at[1])]
+    copies = [pltpu.make_async_copy(src, dst, sem.at[i]) for i, (src, dst) in enumerate(moves)]
+    for copy in copies:
+        copy.start()
+    for copy in copies:
+        copy.wait()
+
+
+def written(current, dual):
+    vmem, hbm = (pl.BlockSpec(memory_space=space) for space in (pltpu.VMEM, pltpu.HBM))
+    return pl.pallas_call(
+        write_kernel,
+        out_shape=tuple(jax.ShapeDtypeStruct(x.shape, x.dtype) for x in (current, dual)),
+        in_specs=[vmem, vmem],
+        out_specs=(hbm, hbm),
+        scratch_shapes=[pltpu.SemaphoreType.DMA((3,))],
+        compiler_params=pltpu.CompilerParams(vmem_limit_bytes=8 * 1024 * 1024),
+    )(current, dual)
+
+
 def solution(mesh):
     n_row, n_col = mesh.shape["row"], mesh.shape["col"]
 
@@ -374,7 +398,7 @@
             + [
                 pltpu.VMEM((LANE, rows), f32),
                 pltpu.VMEM((LANE, rows + 2 * LANE), f32),
-                pltpu.VMEM((ITERS, n_row * n_col, 2, LANE), f32),
+                pltpu.VMEM((ITERS, n_row * n_col, 1, LANE), f32),
                 pltpu.SemaphoreType.DMA((2, 3)),
                 pltpu.SemaphoreType.DMA((10,)),
                 pltpu.SemaphoreType.DMA((10,)),
@@ -386,6 +410,7 @@
                 collective_id=0, has_side_effects=True, vmem_limit_bytes=40 * 1024 * 1024
             ),
         )(*(pltpu.with_memory_space_constraint(x, pltpu.HBM) for x in (noisy, fidelity)))
+        current, dual = written(current, dual)
         return current, dual, tau[0, 0]
 
     return jax.shard_map(

time: 52.3 us -> 50.8 us (0.971)
  local copies, waits for them, and re-layouts: 2.29 us -> 0 us
  Pallas kernels: 48.1 us -> 48.9 us
    unnamed x2 -> x0, local copies, waits for them, and re-layouts: 2.29 us -> none
    pallas_call x0 -> x1, Pallas kernels: none -> 1.69 us  [written(): pl.pallas_call(write_kernel, out_shape=tuple((jax.ShapeDtypeStruct(x.shap...]
    pallas_call x1, Pallas kernels: 48.1 us -> 47.2 us  [on_device(): pl.pallas_call(functools.partial(kernel, n_row, n_col, cells), out_shape=...]
where the time goes in v5:
time: 50.8 us; the launch traced here: 50.7 us
  Pallas kernels  48.9 us (96%)
  between operations  1.8 us (4%)
    pallas_call x1, Pallas kernels, on_device(): pl.pallas_call(functools.partial(kernel, n_row, n_col, cells), out_shape=...  47.2 us
    pallas_call x1, Pallas kernels, written(): pl.pallas_call(write_kernel, out_shape=tuple((jax.ShapeDtypeStruct(x.shap...  1.69 us

profile of v5, /device:TPU:1, one launch (start us, length us, event | category | flops | bytes accessed | tf_op | source)
XLA Modules:
  0.0 50.7 jit_solution(8719323058346153489)
XLA Ops:
  0.6 47.2 %shard_map.49 = (f32[256,1024]{1,0:T(8,128)S(1)}, f32[2,256,1024]{2,1,0:T(8,128)S(1)}, f32[1,128]{1,0:T(1,128)S(1)}) custom-call(f32[256,1024]{1,0:T(8,128)} %noisy_hbm.1, f32[256,1024]{1,0:T(8,128)} %fid_hbm.1), custom_call_target="tpu_custom_call" | custom-call | tf_op jit(solution)/shard_map/pallas_call | solution.py:388
  47.8 1.7 %shard_map.50 = (f32[256,1024]{1,0:T(8,128)}, f32[2,256,1024]{2,1,0:T(8,128)}) custom-call(f32[256,1024]{1,0:T(8,128)S(1)} %get-tuple-element.8.u_ref, f32[2,256,1024]{2,1,0:T(8,128)S(1)} %get-tuple-element.9.dual_ref), custom_call_target="tpu_custom_call" | custom-call | tf_op jit(solution)/shard_map/pallas_call | solution.py:369

commit v6 on v5

--- a/solution.py
+++ b/solution.py
@@ -19,7 +19,7 @@
 
 SUB = 8
 LANE = 128
-UNROLL = 6
+UNROLL = 10
 
 
 def kernel(

time: 50.8 us -> 50.6 us (level)
  no operation moved by 1% of the time
where the time goes in v6:
time: 50.6 us; the launch traced here: 50.5 us
  Pallas kernels  48.7 us (96%)
  between operations  1.8 us (4%)
    pallas_call x1, Pallas kernels, on_device(): pl.pallas_call(functools.partial(kernel, n_row, n_col, cells), out_shape=...  47 us
    pallas_call x1, Pallas kernels, written(): pl.pallas_call(write_kernel, out_shape=tuple((jax.ShapeDtypeStruct(x.shap...  1.69 us

profile of v6, /device:TPU:1, one launch (start us, length us, event | category | flops | bytes accessed | tf_op | source)
XLA Modules:
  0.0 50.5 jit_solution(1416545121893375673)
XLA Ops:
  0.6 47.0 %shard_map.49 = (f32[256,1024]{1,0:T(8,128)S(1)}, f32[2,256,1024]{2,1,0:T(8,128)S(1)}, f32[1,128]{1,0:T(1,128)S(1)}) custom-call(f32[256,1024]{1,0:T(8,128)} %noisy_hbm.1, f32[256,1024]{1,0:T(8,128)} %fid_hbm.1), custom_call_target="tpu_custom_call" | custom-call | tf_op jit(solution)/shard_map/pallas_call | solution.py:388
  47.6 1.7 %shard_map.50 = (f32[256,1024]{1,0:T(8,128)}, f32[2,256,1024]{2,1,0:T(8,128)}) custom-call(f32[256,1024]{1,0:T(8,128)S(1)} %get-tuple-element.8.u_ref, f32[2,256,1024]{2,1,0:T(8,128)S(1)} %get-tuple-element.9.dual_ref), custom_call_target="tpu_custom_call" | custom-call | tf_op jit(solution)/shard_map/pallas_call | solution.py:369

commit v7 on v6

--- a/solution.py
+++ b/solution.py
@@ -23,7 +23,7 @@
 
 
 def kernel(
-    n_row, n_col, cells,
+    n_row, n_col, per_cell,
     noisy_hbm, fid_hbm,
     u_out, dual_out, tau_out,
     N, F, U, H, UB, DU, PX, PY, GX, GY, DV, QT, CB, rb,
@@ -170,13 +170,11 @@
     ]
     pl.semaphore_wait(barrier, len(around))
     tell()
-    for halo in halos[:4]:
-        halo.start()
     for load in edges:
         load.wait()
     for b in range(rows // LANE):
         QT[:, b * LANE : (b + 1) * LANE] = pack(b)
-    for halo in halos[4:]:
+    for halo in halos[6:] + halos[4:6] + halos[:4]:
         halo.start()
     for load in inner:
         load.wait()
@@ -342,7 +340,7 @@
         else:
             over_strips(1, strips - 1, 4, finish)
         primal, dual = reduce_end(k)
-        ratio = jnp.log((primal / cells + epsilon) / (dual / cells + epsilon))
+        ratio = jnp.log((primal * per_cell + epsilon) / (dual * per_cell + epsilon))
         rate = np.float32(adapt_rate * adapt_decay**k)
         tau_one = tau_one * jnp.exp(rate * ratio / (1.0 + jnp.abs(ratio)))
         sigma_one = step_product / tau_one
@@ -383,10 +381,10 @@
         rows, cols = noisy.shape
         f32 = jnp.float32
         padded = pltpu.VMEM((rows + 2 * SUB, cols + LANE), f32)
-        cells = np.float32(rows * cols * n_row * n_col)
+        per_cell = np.float32(1.0 / (rows * cols * n_row * n_col))
         vmem = pl.BlockSpec(memory_space=pltpu.VMEM)
         current, dual, tau = pl.pallas_call(
-            functools.partial(kernel, n_row, n_col, cells),
+            functools.partial(kernel, n_row, n_col, per_cell),
             out_shape=(
                 jax.ShapeDtypeStruct((rows, cols), f32),
                 jax.ShapeDtypeStruct((2, rows, cols), f32),

time: 50.6 us -> 50.6 us (level)
  no operation moved by 1% of the time
where the time goes in v7:
time: 50.6 us; the launch traced here: 50.4 us
  Pallas kernels  48.6 us (96%)
  between operations  1.8 us (4%)
    pallas_call x1, Pallas kernels, on_device(): pl.pallas_call(functools.partial(kernel, n_row, n_col, per_cell), out_sha...  46.9 us
    pallas_call x1, Pallas kernels, written(): pl.pallas_call(write_kernel, out_shape=tuple((jax.ShapeDtypeStruct(x.shap...  1.69 us

profile of v7, /device:TPU:1, one launch (start us, length us, event | category | flops | bytes accessed | tf_op | source)
XLA Modules:
  0.0 50.4 jit_solution(146385562766219329)
XLA Ops:
  0.6 46.9 %shard_map.49 = (f32[256,1024]{1,0:T(8,128)S(1)}, f32[2,256,1024]{2,1,0:T(8,128)S(1)}, f32[1,128]{1,0:T(1,128)S(1)}) custom-call(f32[256,1024]{1,0:T(8,128)} %noisy_hbm.1, f32[256,1024]{1,0:T(8,128)} %fid_hbm.1), custom_call_target="tpu_custom_call" | custom-call | tf_op jit(solution)/shard_map/pallas_call | solution.py:386
  47.6 1.7 %shard_map.50 = (f32[256,1024]{1,0:T(8,128)}, f32[2,256,1024]{2,1,0:T(8,128)}) custom-call(f32[256,1024]{1,0:T(8,128)S(1)} %get-tuple-element.8.u_ref, f32[2,256,1024]{2,1,0:T(8,128)S(1)} %get-tuple-element.9.dual_ref), custom_call_target="tpu_custom_call" | custom-call | tf_op jit(solution)/shard_map/pallas_call | solution.py:367
